TPU v7x, 32 devices: a whole 2x2x4 slice. The times are simulated.
32 devices in a mesh: grp: 2 (over y), seq: 16 (over z, x, core).
Axes of the slice: x: 2, y: 2, z: 4, core: 2. Of those that a mesh axis runs over, the one named last changes fastest.
Arguments:
- gate_out: bfloat16 [8192, 4096], P(('grp', 'seq')), parts along dimension 0, may hold values from -6 to 6
- gate_in: bfloat16 [8192, 4096], P(('grp', 'seq')), parts along dimension 0, may hold values from -6 to 6
- values: bfloat16 [8192, 4096], P(('grp', 'seq')), parts along dimension 0, may hold values from -6 to 6
- gate_mid: bfloat16 [8192, 4096], P(('grp', 'seq')), parts along dimension 0, may hold values from -6 to 6
- medium_taps: bfloat16 [256, 128], replicated, may hold values from -0.5 to 0.5
- medium_skip: float32 [4096], replicated, may hold values from -3 to 3
- residues: float32 [256, 16], replicated, may hold values from -1 to 1, as said below
- rates: float32 [256, 16], replicated, may hold values from 0 to 0.1, as said below
- long_skip: float32 [4096], replicated, may hold values from -3 to 3
Outputs:
- mixed: bfloat16 [8192, 4096], P(('grp', 'seq')), parts along dimension 0
There are 2 independent parts, one for each index of `grp`. A program takes and returns all parts, laid end to end along the dimension named above; an argument that names none is the same for every part. Nothing has to cross between parts.
Inputs may be any that keep to these rules, and one draw needn't show every extreme that they name: Positive rates; each pole's filter falls by exp(-rate) per position. Real residues of the poles.
All inputs are finite; a program needn't handle non-finite values.
Results may differ from a plain program's by a relative error of at most 0.0061.
Values may be sent and summed in bfloat16 or wider, within the bound.
No kernel may reach another device: no remote copies, remote signals or barrier semaphores. Data moves between devices by JAX's collectives and lax.ppermute only.
A program may use at most 192 MiB of HBM per device.

v0:
```python
import jax
import jax.numpy as jnp
from jax import lax
from jax.sharding import PartitionSpec as P

MED = 128
SUB = 128


def from_behind(block, axis, distance):
    devices = range(lax.axis_size(axis))
    route = [(i - distance, i) for i in devices if i - distance in devices]
    return lax.ppermute(block, axis, route)


def banded(tap_values, out_rows, in_cols):
    group_count, tap_count = tap_values.shape
    line = jnp.concatenate(
        [
            jnp.zeros((group_count, in_cols - tap_count), tap_values.dtype),
            tap_values[:, ::-1],
            jnp.zeros((group_count, out_rows - 1), tap_values.dtype),
        ],
        axis=1,
    )
    cycle = jnp.concatenate(
        [
            line[:, out_rows - 1 :],
            jnp.zeros((group_count, 1), tap_values.dtype),
            line[:, : out_rows - 1],
        ],
        axis=1,
    )
    period = cycle.shape[1]
    tiled = jnp.tile(cycle, (1, out_rows))[:, : out_rows * (period - 1)]
    return tiled.reshape(group_count, out_rows, period - 1)[:, :, :in_cols]


def link_flat(earlier, latter):
    return (earlier[0] * latter[0], latter[0] * earlier[1] + latter[1])


def shards(
    gate_out, gate_in, values, gate_mid, medium_taps, medium_skip, residues, rates, long_skip
):
    row_count, feature_count = gate_out.shape
    group_count, pole_count = rates.shape
    group_width = feature_count // group_count
    block_count = row_count // SUB
    lane_rows = group_width * block_count
    maximum_level = lax.Precision.HIGHEST
    product = (gate_in.astype(jnp.float32) * values.astype(jnp.float32)).astype(jnp.bfloat16)
    rim_rows = from_behind(product[row_count - (MED - 1) :], "seq", 1)
    product_cols = product.T
    previous_cols = jnp.concatenate(
        [
            jnp.zeros((feature_count, SUB - MED + 1), jnp.bfloat16),
            rim_rows.T,
            product_cols[:, : row_count - SUB],
        ],
        axis=1,
    )
    sliding_spans = jnp.concatenate(
        [
            previous_cols.reshape(group_count, lane_rows, SUB),
            product_cols.reshape(group_count, lane_rows, SUB),
        ],
        axis=2,
    )
    middle_filter_matrix = banded(medium_taps, SUB, 2 * SUB)
    medium_conv = jnp.einsum(
        "lkw,lyw->lyk", middle_filter_matrix, sliding_spans, preferred_element_type=jnp.float32
    ).reshape(feature_count, row_count)
    medium = medium_conv + medium_skip[:, None] * product_cols.astype(jnp.float32)
    gated_cols = (gate_mid.T.astype(jnp.float32) * medium).astype(jnp.bfloat16)
    gate_product_block = gated_cols.reshape(group_count, lane_rows, SUB)
    offsets = jnp.arange(SUB).astype(jnp.float32)
    decay_up = jnp.exp(-rates[:, :, None] * offsets)
    long_taps = jnp.einsum("gp,gpn->gn", residues, decay_up, precision=maximum_level).astype(
        jnp.bfloat16
    )
    short_filter_matrix = banded(long_taps, SUB, SUB)
    fold_weights = jnp.exp(-rates[:, :, None] * (SUB - 1.0 - offsets)).astype(jnp.bfloat16)
    sub_states = jnp.einsum(
        "gps,grs->gpr", fold_weights, gate_product_block, preferred_element_type=jnp.float32
    )
    sub_states = sub_states.reshape(group_count, pole_count, group_width, block_count)
    powers = jnp.broadcast_to(jnp.exp(-rates * SUB)[:, :, None, None], sub_states.shape)
    _, inclusive = lax.associative_scan(link_flat, (powers, sub_states), axis=3)
    summary = inclusive[:, :, :, block_count - 1]
    device_power = jnp.exp(-rates * (SUB * block_count))
    device_count = lax.axis_size("seq")
    flat_states = summary.reshape(1, -1)
    slice_width = flat_states.shape[1] // device_count
    spread_states = lax.all_to_all(flat_states, "seq", split_axis=1, concat_axis=0, tiled=True)
    power_flat = jnp.broadcast_to(device_power[:, :, None], summary.shape).reshape(-1)
    own_powers = lax.dynamic_slice_in_dim(
        power_flat, lax.axis_index("seq") * slice_width, slice_width
    )
    stacked_powers = jnp.broadcast_to(own_powers[None], (device_count, slice_width))
    _, running = lax.associative_scan(link_flat, (stacked_powers, spread_states))
    shifted = jnp.concatenate([jnp.zeros_like(running[:1]), running[: device_count - 1]], axis=0)
    carry_in = lax.all_to_all(shifted, "seq", split_axis=0, concat_axis=1, tiled=True).reshape(
        summary.shape
    )
    intra_part = jnp.einsum(
        "lkw,lyw->lyk", short_filter_matrix, gate_product_block, preferred_element_type=jnp.float32
    )
    block_ages = jnp.arange(block_count).astype(jnp.float32)
    lifted = jnp.exp(-rates[:, :, None, None] * (SUB * block_ages[None, None, None, :]))
    exclusive = jnp.concatenate(
        [jnp.zeros_like(inclusive[:, :, :, :1]), inclusive[:, :, :, : block_count - 1]], axis=3
    )
    preceding_rows = (lifted * carry_in[:, :, :, None] + exclusive).reshape(
        group_count, pole_count, lane_rows
    )
    distance_weight = residues[:, :, None] * jnp.exp(-rates[:, :, None] * (offsets + 1.0))
    previous_portion = jnp.einsum(
        "izo,iza->iao", distance_weight, preceding_rows, precision=maximum_level
    )
    long_cols = (intra_part + previous_portion).reshape(feature_count, row_count) + long_skip[
        :, None
    ] * gated_cols.astype(jnp.float32)
    return (gate_out.astype(jnp.float32) * long_cols.T).astype(jnp.bfloat16)


def solution(mesh):
    in_specs = (
        P(("grp", "seq"), None),
        P(("grp", "seq"), None),
        P(("grp", "seq"), None),
        P(("grp", "seq"), None),
        P(),
        P(),
        P(),
        P(),
        P(),
    )
    out_specs = P(("grp", "seq"), None)
    return jax.shard_map(shards, mesh=mesh, in_specs=in_specs, out_specs=out_specs, check_vma=False)
```

profile of v0, /device:TPU:0, one launch (start us, length us, event | category | flops | bytes accessed | tf_op | source)
XLA Modules:
  0.0 357.6 jit_solution(16840898267158692840)
XLA Ops:
  0.0 3.0 multiply_convert_fusion
  4.3 3.4 collective-permute-start
  10.7 2.6 copy.32
  14.9 3.5 tile.8
  18.4 21.8 %copy.48 = bf16[32,8,128,384]{3,1,2,0:T(8,128)(2,1)} copy(bf16[32,8,128,384]{3,2,1,0:T(8,128)(2,1)S(1)} %bitcast.38) | data formatting | bytes 50331648
  40.3 20.6 %slice.177 = bf16[256,49024]{1,0:T(8,128)(2,1)} slice(bf16[256,49152]{1,0:T(8,128)(2,1)} %bitcast.39), slice={[0:256], [0:49024]} | slice | bytes 50200576 | tf_op jit(solution)/shard_map/slice | solution.py:35
  60.8 59.8 %reshape.93 = bf16[256,128,383]{2,1,0:T(8,128)(2,1)} reshape(bf16[256,49024]{1,0:T(8,128)(2,1)} %slice.177) | data formatting | bytes 50200576 | tf_op jit(solution)/shard_map/reshape | solution.py:36
  120.6 4.1 %reshape.92 = bf16[256,32,128]{2,1,0:T(8,128)(2,1)} reshape(bf16[4096,256]{1,0:T(8,128)(2,1)} %copy.32) | data formatting | bytes 4194304 | tf_op jit(solution)/shard_map/reshape | solution.py:66
  126.9 2.8 reshape.98
  133.6 3.2 pad_maximum_fusion
  136.8 4.1 %copy.31 = bf16[4096,256]{1,0:T(8,128)(2,1)} copy(bf16[4096,256]{0,1:T(8,128)(2,1)} %pad_maximum_fusion) | data formatting | bytes 4194304 | tf_op jit(solution)/shard_map/concatenate | solution.py:55
  140.9 4.1 %reshape.91 = bf16[256,32,128]{2,1,0:T(8,128)(2,1)} reshape(bf16[4096,256]{1,0:T(8,128)(2,1)} %copy.31) | data formatting | bytes 4194304 | tf_op jit(solution)/shard_map/reshape | solution.py:65
  144.9 11.3 %fusion = f32[256,32,128]{2,1,0:T(8,128)} fusion(bf16[256,128,383]{2,1,0:T(8,128)(2,1)} %reshape.93, bf16[256,32,128]{2,1,0:T(8,128)(2,1)} %reshape.92, bf16[256,32,128]{2,1,0:T(8,128)(2,1)} %reshape.91), kind=kOutput, calls=%fused_computation | convolution fusion | flops 545259520 | bytes 25165824 | tf_op jit(solution)/shard_map/lkw,lyw->lyk/dot_general | solution.py:71
  156.3 5.2 %reshape.94 = f32[4096,256]{1,0:T(8,128)} reshape(f32[256,32,128]{2,1,0:T(8,128)} %fusion) | data formatting | bytes 8388608 | tf_op jit(solution)/shard_map/reshape | solution.py:73
  161.4 5.6 %copy.33 = f32[4096,256]{0,1:T(8,128)} copy(f32[4096,256]{1,0:T(8,128)} %reshape.94) | data formatting | bytes 8388608 | tf_op jit(solution)/shard_map/reshape | solution.py:73
  167.1 5.0 %fusion.8 = bf16[4096,256]{0,1:T(8,128)(2,1)} fusion(bf16[256,4096]{1,0:T(8,128)(2,1)} %param.12, f32[4096,256]{0,1:T(8,128)} %copy.33, f32[4096]{0:T(1024)S(1)} %copy-done.12, bf16[256,4096]{1,0:T(8,128)(2,1)S(1)} %multiply_convert_fusion), kind=kLoop, calls=%fused_computation.10 | loop fusion | flops 6291456 | bytes 10502144 | tf_op jit(solution)/shard_map/convert_element_type | solution.py:75
  172.1 4.1 %copy.34 = bf16[4096,256]{1,0:T(8,128)(2,1)} copy(bf16[4096,256]{0,1:T(8,128)(2,1)} %fusion.8) | data formatting | bytes 4194304 | tf_op jit(solution)/shard_map/convert_element_type | solution.py:75
  176.2 2.7 reshape.95
  178.9 2.4 fusion.15
  181.3 2.7 copy.36
  184.1 2.5 copy.37
  186.6 3.0 all_to_all.27
  189.6 6.2 %all-to-all-start = ((f32[1,16,4096]{2,0,1:T(1,128)}), f32[1,16,4096]{2,0,1:T(1,128)S(1)}, u32[]{:S(2)}, u32[]{:S(2)}) async-start(f32[1,16,4096]{2,0,1:T(1,128)} %all_to_all.27), calls=%async_computation | async-start | bytes 524288 | tf_op jit(solution)/shard_map/all_to_all | solution.py:95
  198.5 41.7 %copy.49 = bf16[32,8,128,256]{3,1,2,0:T(8,128)(2,1)S(1)} copy(bf16[32,8,128,256]{3,2,1,0:T(8,128)(2,1)S(1)} %bitcast.40) | data formatting | bytes 33554432
  240.2 6.6 %slice.180 = bf16[256,32640]{1,0:T(8,128)(2,1)} slice(bf16[256,32768]{1,0:T(8,128)(2,1)S(1)} %bitcast.41), slice={[0:256], [0:32640]} | slice | bytes 33423360 | tf_op jit(solution)/shard_map/slice | solution.py:35
  246.8 56.7 %reshape.96 = bf16[256,128,255]{2,1,0:T(8,128)(2,1)} reshape(bf16[256,32640]{1,0:T(8,128)(2,1)} %slice.180) | data formatting | bytes 33423360 | tf_op jit(solution)/shard_map/reshape | solution.py:36
  310.6 6.0 %all-to-all-start.1 = ((f32[16,1,4096]{2,1,0:T(1,128)}), f32[16,1,4096]{2,1,0:T(1,128)S(1)}, u32[]{:S(2)}, u32[]{:S(2)}) async-start(f32[16,1,4096]{2,1,0:T(1,128)} %copy.40), calls=%async_computation.1 | async-start | bytes 524288 | tf_op jit(solution)/shard_map/all_to_all | solution.py:103
  316.6 9.8 %fusion.2 = f32[256,32,128]{2,1,0:T(8,128)} fusion(bf16[256,32,128]{2,1,0:T(8,128)(2,1)S(1)} %reshape.95, bf16[256,128,255]{2,1,0:T(8,128)(2,1)} %reshape.96), kind=kOutput, calls=%fused_computation.2 | convolution fusion | flops 268435456 | bytes 14680064 | tf_op jit(solution)/shard_map/lkw,lyw->lyk/dot_general | solution.py:106
  330.6 10.9 %convolution_add_fusion = f32[256,32,128]{2,1,0:T(8,128)} fusion(f32[256,32,128]{2,1,0:T(8,128)} %fusion.2, f32[256,16,32]{2,1,0:T(8,128)S(1)} %copy.43, f32[128]{0:T(128)S(1)} %copy-done.15, f32[256,16]{1,0:T(8,128)S(1)} %copy-done.1, f32[256,16]{1,0:T(8,128)S(1)} %copy.35), kind=kOutput, calls=%fused_computation.12 | convolution fusion | flops 203423744 | bytes 8946176 | tf_op jit(solution)/shard_map/izo,iza->iao/dot_general | solution.py:118
  341.6 5.2 %reshape.100 = f32[4096,256]{1,0:T(8,128)} reshape(f32[256,32,128]{2,1,0:T(8,128)} %convolution_add_fusion) | data formatting | bytes 8388608 | tf_op jit(solution)/shard_map/reshape | solution.py:121
  346.8 5.8 %copy.44 = f32[4096,256]{0,1:T(8,128)} copy(f32[4096,256]{1,0:T(8,128)} %reshape.100) | data formatting | bytes 8388608 | tf_op jit(solution)/shard_map/reshape | solution.py:121
  352.5 5.1 %fusion.7 = bf16[256,4096]{1,0:T(8,128)(2,1)} fusion(f32[4096,256]{0,1:T(8,128)} %copy.44, bf16[4096,256]{0,1:T(8,128)(2,1)S(1)} %copy-done, bf16[256,4096]{1,0:T(8,128)(2,1)} %param.9, f32[4096]{0:T(1024)S(1)} %copy-done.13), kind=kLoop, calls=%fused_computation.8 | loop fusion | flops 6291456 | bytes 10502144 | tf_op jit(solution)/shard_map/convert_element_type | solution.py:124
  (110 shorter events, 25.6 us)
Async XLA Ops:
  3.0 4.6 %copy-start.9 = (f32[256,16]{0,1:T(8,128)S(1)}, f32[256,16]{0,1:T(8,128)}, u32[]{:S(2)}) copy-start(f32[256,16]{0,1:T(8,128)} %param.15) | copy-start | bytes 49156
  3.0 4.7 %copy-start.14 = (f32[256,16]{0,1:T(8,128)S(1)}, f32[256,16]{0,1:T(8,128)}, u32[]{:S(2)}) copy-start(f32[256,16]{0,1:T(8,128)} %param.16) | copy-start | bytes 49156
  4.3 129.3 %collective-permute-start = (bf16[127,4096]{1,0:T(8,128)(2,1)}, bf16[127,4096]{1,0:T(8,128)(2,1)}, u32[]{:S(2)}, u32[]{:S(2)}) collective-permute-start(bf16[127,4096]{1,0:T(8,128)(2,1)} %slice.174), channel_id=1, source_target_pairs={{0,1},{1,2},{2,3},{3,4},{4,5},{5,6},{6,7},{7,8},{8,9},{9,10},{10,1... | collective-permute-start | bytes 3121160 | tf_op jit(solution)/shard_map/ppermute | solution.py:13
  8.4 2.3 copy-start.4
  13.4 1.0 copy-start.11
  126.9 5.8 %copy-start.3 = (bf16[256,128]{1,0:T(8,128)(2,1)S(1)}, bf16[256,128]{1,0:T(8,128)(2,1)}, u32[]{:S(2)}) copy-start(bf16[256,128]{1,0:T(8,128)(2,1)} %rev.7) | copy-start | bytes 196612
  161.4 5.6 %copy-start.12 = (f32[4096]{0:T(1024)S(1)}, f32[4096]{0:T(1024)}, u32[]{:S(2)}) copy-start(f32[4096]{0:T(1024)} %param.14) | copy-start | bytes 49156
  176.2 2.7 copy-start.17
  181.3 2.7 copy-start.8
  184.1 12.4 %copy-start.10 = (f32[256,16]{0,1:T(8,128)S(1)}, f32[256,16]{0,1:T(8,128)}, u32[]{:S(2)}) copy-start(f32[256,16]{0,1:T(8,128)} %param.15) | copy-start | bytes 49156
  186.6 10.6 %copy-start.2 = (bf16[256,256]{1,0:T(8,128)(2,1)S(1)}, bf16[256,256]{1,0:T(8,128)(2,1)}, u32[]{:S(2)}) copy-start(bf16[256,256]{1,0:T(8,128)(2,1)} %pad_maximum_fusion.4) | copy-start | bytes 393220
  189.6 115.1 %all-to-all-start = ((f32[1,16,4096]{2,0,1:T(1,128)}), f32[1,16,4096]{2,0,1:T(1,128)S(1)}, u32[]{:S(2)}, u32[]{:S(2)}) async-start(f32[1,16,4096]{2,0,1:T(1,128)} %all_to_all.27), calls=%async_computation | async-start | bytes 524288 | tf_op jit(solution)/shard_map/all_to_all | solution.py:95
  246.8 57.3 %copy-start.5 = (f32[256,16]{0,1:T(8,128)S(1)}, f32[256,16]{0,1:T(8,128)}, u32[]{:S(2)}) copy-start(f32[256,16]{0,1:T(8,128)} %copy-done.4) | copy-start | bytes 49156
  246.8 57.3 %copy-start.16 = (f32[2]{0:T(128)S(1)}, f32[2]{0:T(128)}, u32[]{:S(2)}) copy-start(f32[2]{0:T(128)} %convert_multiply_fusion) | copy-start | bytes 28
  304.1 1.6 copy-start.6
  310.6 16.0 %all-to-all-start.1 = ((f32[16,1,4096]{2,1,0:T(1,128)}), f32[16,1,4096]{2,1,0:T(1,128)S(1)}, u32[]{:S(2)}, u32[]{:S(2)}) async-start(f32[16,1,4096]{2,1,0:T(1,128)} %copy.40), calls=%async_computation.1 | async-start | bytes 524288 | tf_op jit(solution)/shard_map/all_to_all | solution.py:103
  327.2 1.9 copy-start.7
  329.1 1.5 copy-start.1
  329.1 1.5 copy-start.15
  346.8 5.8 %copy-start = (bf16[4096,256]{0,1:T(8,128)(2,1)S(1)}, bf16[4096,256]{0,1:T(8,128)(2,1)}, u32[]{:S(2)}) copy-start(bf16[4096,256]{0,1:T(8,128)(2,1)} %fusion.8) | copy-start | bytes 6291460
  346.8 5.8 %copy-start.13 = (f32[4096]{0:T(1024)S(1)}, f32[4096]{0:T(1024)}, u32[]{:S(2)}) copy-start(f32[4096]{0:T(1024)} %param.17) | copy-start | bytes 49156
where the time goes:
time: 359 us; the launch traced here: 358 us
  local copies, waits for them, and re-layouts  278 us (77%)
  matrix products  36.7 us (10%)
  other arithmetic  26.3 us (7%)
  starting transfers between devices  15.6 us (4%)
    reshape x2, local copies, waits for them, and re-layouts, banded(): return tiled.reshape(group_count, out_rows, period - 1)[:, :, :in_cols]  116 us
    unnamed x42, local copies, waits for them, and re-layouts  64.7 us
    slice x2, local copies, waits for them, and re-layouts, banded(): tiled = jnp.tile(cycle, (1, out_rows))[:, :out_rows * (period - 1)]  27.1 us
    dot_general x1, matrix products, shards(): jnp.einsum('lkw,lyw->lyk', middle_filter_matrix, sliding_spans, preferred...  11.3 us
    reshape x2, local copies, waits for them, and re-layouts, shards(): (intra_part + previous_portion).reshape(feature_count, row_count)  11 us
    dot_general x1, matrix products, shards(): jnp.einsum('izo,iza->iao', distance_weight, preceding_rows, precision=max...  10.9 us
    reshape x2, local copies, waits for them, and re-layouts, shards(): medium_conv = jnp.einsum('lkw,lyw->lyk', middle_filter_matrix, sliding_sp...  10.8 us
    dot_general x1, matrix products, shards(): jnp.einsum('lkw,lyw->lyk', short_filter_matrix, gate_product_block, prefe...  9.81 us
  transfers between devices with their start and end apart: 3, of which 1 were waited for; matrix products, arithmetic and copies ran while one was open for 68% of the time, Pallas kernels for 0%

commit v1 on v0

v1 whole, which is shorter than its diff:
```python
import functools

import jax
import jax.numpy as jnp
from jax import lax
from jax.experimental import pallas as pl
from jax.experimental.pallas import tpu as pltpu
from jax.sharding import PartitionSpec as P

MED = 128
SUB = 128
STRIP = 32
LANES = 128
WIDE = 256
BF16 = jnp.bfloat16
F32 = jnp.float32


def dot(a, b, precision=None):
    return jnp.dot(a, b, preferred_element_type=F32, precision=precision)


def own_groups(stack, rows, per_group):
    groups = stack.shape[0] // rows
    owner = lax.broadcasted_iota(jnp.int32, (rows, stack.shape[1]), 1) % LANES // per_group
    kept = stack[:rows]
    for g in range(1, groups):
        kept = jnp.where(owner == g, stack[g * rows : (g + 1) * rows], kept)
    return kept


def toeplitz(line, g):
    spread = jnp.broadcast_to(line[g : g + 1], (STRIP, 2 * LANES))
    return pltpu.roll(spread, 0, 1, stride=1, stride_axis=0)


def pair_of_strips(window, start, depth, lanes):
    return jnp.concatenate(
        [window[start : start + depth, lanes], window[start + STRIP : start + STRIP + depth, lanes]],
        axis=1,
    )


def medium_block(strips, window, lanes, per_group, out):
    for i in range(0, SUB // STRIP, 2):
        spans = pair_of_strips(window, i * STRIP, MED + STRIP, lanes)
        both = own_groups(dot(strips, spans), STRIP, per_group)
        out[i * STRIP : (i + 1) * STRIP, lanes] = both[:, :LANES]
        out[(i + 1) * STRIP : (i + 2) * STRIP, lanes] = both[:, LANES:]


def inner_block(strips, window, lanes, per_group, out):
    for i in range(0, SUB // STRIP, 2):
        spans = pair_of_strips(window, i * STRIP, SUB, lanes)
        both = own_groups(dot(strips, spans), STRIP, per_group)
        out[i * STRIP : (i + 1) * STRIP, lanes] = both[:, :LANES]
        out[(i + 1) * STRIP : (i + 2) * STRIP, lanes] = both[:, LANES:]


def early_kernel(
    per_group, poles,
    gate_in, values, gate_mid, taps, rates, residues, med_skip, long_skip,
    med_strips, long_strips, folds, rates_pc, part, state,
    window, padded, work,
):
    step = pl.program_id(0)
    block = LANES // per_group
    window[...] = (gate_in[...].astype(F32) * values[...].astype(F32)).astype(BF16)
    tap = lax.broadcasted_iota(jnp.int32, (LANES, 2 * LANES), 0)
    spot = lax.broadcasted_iota(jnp.int32, (LANES, 2 * LANES), 1)
    med_line = dot(taps[...], (spot == MED - tap).astype(BF16))
    long_turn = (spot == (SUB - STRIP - tap) % (2 * LANES)).astype(BF16)
    offset = lax.broadcasted_iota(jnp.int32, (LANES, LANES), 1).astype(F32)
    padded[: SUB - STRIP] = jnp.zeros((SUB - STRIP, WIDE), BF16)
    for b in range(WIDE // LANES):
        lanes = slice(b * LANES, (b + 1) * LANES)
        row = step * (WIDE // LANES) + b
        rate_row = rates[pl.ds(row, 1), :]
        residue_row = residues[pl.ds(row, 1), :]
        rate_col = jnp.transpose(jnp.broadcast_to(rate_row, (LANES, LANES)))
        rates_pc[:, lanes] = own_groups(rate_col, poles, per_group)
        decay_up = jnp.exp(-rate_col * offset)
        owner = lax.broadcasted_iota(jnp.int32, (block, LANES), 1) // poles
        mine = lax.broadcasted_iota(jnp.int32, (block, LANES), 0)
        spread = jnp.where(owner == mine, jnp.broadcast_to(residue_row, (block, LANES)), 0.0)
        long_line = dot(
            dot(spread, decay_up, lax.Precision.HIGHEST).astype(BF16), long_turn
        )
        folds[lanes, :] = jnp.exp(-rate_col * (SUB - 1.0 - offset)).astype(BF16)
        for g in range(block):
            rows = slice((b * block + g) * STRIP, (b * block + g + 1) * STRIP)
            med_strips[rows, :] = toeplitz(med_line, b * block + g)[:, : MED + STRIP].astype(BF16)
            long_strips[rows, :] = toeplitz(long_line, g)[:, :LANES].astype(BF16)
        strips = slice(b * block * STRIP, (b + 1) * block * STRIP)
        medium_block(med_strips[strips, :], window, lanes, per_group, work)
        medium = work[:, lanes] + med_skip[:, lanes] * window[SUB:, lanes].astype(F32)
        gated = (gate_mid[:, lanes].astype(F32) * medium).astype(BF16)
        padded[SUB - STRIP :, lanes] = gated
        state[:, lanes] = own_groups(dot(folds[lanes, :], gated), poles, per_group)
        inner_block(long_strips[strips, :], padded, lanes, per_group, part)
        part[:, lanes] = part[:, lanes] + long_skip[:, lanes] * gated.astype(F32)


def late_kernel(
    per_group, poles,
    halo_a, halo_b, gate_in, values, gate_mid, med_strips, folds, rates_pc, med_skip, later,
    gated_out, state, total, message,
    window, work,
):
    block = LANES // per_group
    window[:SUB] = halo_a[...] + halo_b[...]
    window[SUB:] = (gate_in[...].astype(F32) * values[...].astype(F32)).astype(BF16)
    for b in range(WIDE // LANES):
        lanes = slice(b * LANES, (b + 1) * LANES)
        strips = slice(b * block * STRIP, (b + 1) * block * STRIP)
        medium_block(med_strips[strips, :], window, lanes, per_group, work)
        medium = work[:, lanes] + med_skip[:, lanes] * window[SUB:, lanes].astype(F32)
        gated = (gate_mid[:, lanes].astype(F32) * medium).astype(BF16)
        gated_out[:, lanes] = gated
        first = own_groups(dot(folds[lanes, :], gated), poles, per_group)
        state[:, lanes] = first
        whole = jnp.exp(-rates_pc[:, lanes] * SUB) * first + later[:, lanes]
        total[:, lanes] = whole
        message[:, lanes] = whole.astype(BF16)


def inner_kernel(
    per_group, poles,
    gated, long_strips, rates, residues, long_skip,
    part, lift,
    padded,
):
    step = pl.program_id(0)
    block = LANES // per_group
    padded[: SUB - STRIP] = jnp.zeros((SUB - STRIP, WIDE), BF16)
    padded[SUB - STRIP :] = gated[...]
    after = lax.broadcasted_iota(jnp.int32, (SUB, LANES), 0).astype(F32) + 1.0
    for b in range(WIDE // LANES):
        lanes = slice(b * LANES, (b + 1) * LANES)
        row = step * (WIDE // LANES) + b
        lift[:, lanes] = (
            residues[pl.ds(row, 1), :] * jnp.exp(-rates[pl.ds(row, 1), :] * after)
        ).astype(BF16)
        strips = slice(b * block * STRIP, (b + 1) * block * STRIP)
        inner_block(long_strips[strips, :], padded, lanes, per_group, part)
        part[:, lanes] = part[:, lanes] + long_skip[:, lanes] * gated[:, lanes].astype(F32)


def spread_groups(state, per_group, poles):
    tall = jnp.concatenate([state] * (LANES // per_group), axis=0)
    owner = lax.broadcasted_iota(jnp.int32, tall.shape, 1) // per_group
    mine = lax.broadcasted_iota(jnp.int32, tall.shape, 0) // poles
    return jnp.where(owner == mine, tall, 0.0).astype(BF16)


def final_kernel(
    per_group, poles, carry, state, rates_pc, lift, part_a, part_b, gate_out, mixed
):
    for b in range(WIDE // LANES):
        lanes = slice(b * LANES, (b + 1) * LANES)
        start = carry[:, lanes]
        middle = jnp.exp(-rates_pc[:, lanes] * SUB) * start + state[:, lanes]
        before = jnp.concatenate(
            [spread_groups(start, per_group, poles), spread_groups(middle, per_group, poles)],
            axis=1,
        )
        lifted = dot(lift[:, lanes], before)
        for part, rows, own in (
            (part_a, slice(0, SUB), slice(0, LANES)),
            (part_b, slice(SUB, 2 * SUB), slice(LANES, 2 * LANES)),
        ):
            long_out = part[:, lanes] + lifted[:, own]
            mixed[rows, lanes] = (gate_out[rows, lanes].astype(F32) * long_out).astype(BF16)


def cols(rows, first=0):
    return pl.BlockSpec((rows, WIDE), lambda j: (first, j))


def tall(rows, width):
    return pl.BlockSpec((rows, width), lambda j: (j, 0))


def fixed(shape):
    return pl.BlockSpec(shape, lambda j: (0, 0))


def call(kernel, grid, in_specs, outs, scratch, name, flops, args):
    moved = sum(a.size * a.dtype.itemsize for a in args)
    moved += sum(s.size * s.dtype.itemsize for s, _ in outs)
    return pl.pallas_call(
        kernel,
        grid=(grid,),
        in_specs=in_specs,
        out_specs=[spec for _, spec in outs],
        out_shape=[shape for shape, _ in outs],
        scratch_shapes=scratch,
        compiler_params=pltpu.CompilerParams(
            dimension_semantics=("arbitrary",), vmem_limit_bytes=24 << 20
        ),
        cost_estimate=pl.CostEstimate(flops=flops, bytes_accessed=moved, transcendentals=0),
        name=name,
    )(*args)


def swap(value, distance):
    count = lax.axis_size("seq")
    route = [(i, i ^ distance) for i in range(count) if i ^ distance < count]
    return lax.ppermute(value, "seq", route)


def scan_states(total, message, rates_pc, positions):
    count = lax.axis_size("seq")
    index = lax.axis_index("seq")
    upper = index % 2 == 1
    features = total.shape[1]
    half = features // 2
    partner = swap(message, 1).astype(F32)
    decay = jnp.exp(-rates_pc * positions)
    chip = decay * jnp.where(upper, partner, total) + jnp.where(upper, total, partner)
    start = jnp.where(upper, half, 0)
    chip = lax.dynamic_slice_in_dim(chip, start, half, axis=1)
    rates = lax.dynamic_slice_in_dim(rates_pc, start, half, axis=1)
    before = jnp.zeros_like(chip)
    size = 2
    while size < count:
        theirs = swap(chip.astype(BF16), size).astype(F32)
        above = (index // size) % 2 == 1
        behind = (index % size) // 2 * 2 * positions
        before += jnp.where(above, jnp.exp(-rates * behind.astype(F32)) * theirs, 0.0)
        chip = jnp.exp(-rates * (positions * size)) * jnp.where(above, theirs, chip) + jnp.where(
            above, chip, theirs
        )
        size *= 2
    before = before.astype(BF16)
    other = swap(before, 1)
    carry = jnp.concatenate(
        [jnp.where(upper, other, before), jnp.where(upper, before, other)], axis=1
    ).astype(F32)
    return jnp.where(upper, decay * carry + partner, carry)


def shards(
    gate_out, gate_in, values, gate_mid, medium_taps, medium_skip, residues, rates, long_skip
):
    row_count, features = gate_out.shape
    groups, poles = rates.shape
    per_group = features // groups
    count = lax.axis_size("seq")
    steps = features // WIDE
    strip_rows = WIDE // per_group * STRIP
    shape = jax.ShapeDtypeStruct

    tail = (gate_in[row_count - SUB :].astype(F32) * values[row_count - SUB :].astype(F32)).astype(
        BF16
    )
    halo_b = lax.ppermute(tail, "seq", [(i, i + 1) for i in range(1, count - 1, 2)])
    halo_a = lax.ppermute(tail, "seq", [(i, i + 1) for i in range(0, count - 1, 2)])

    rate_rows = rates.reshape(-1, LANES)
    residue_rows = residues.reshape(-1, LANES)
    table = fixed(rate_rows.shape)
    med_skip = medium_skip[None]
    lng_skip = long_skip[None]
    all_strips = groups * STRIP

    med_strips, long_strips, folds, rates_pc, part_b, later = call(
        functools.partial(early_kernel, per_group, poles),
        steps,
        [cols(row_count), cols(row_count), cols(SUB, 1), tall(WIDE // per_group, MED), table, table, cols(1), cols(1)],
        [
            (shape((all_strips, MED + STRIP), BF16), tall(strip_rows, MED + STRIP)),
            (shape((all_strips, SUB), BF16), tall(strip_rows, SUB)),
            (shape((groups * poles, SUB), BF16), tall(WIDE // per_group * poles, SUB)),
            (shape((poles, features), F32), cols(poles)),
            (shape((SUB, features), F32), cols(SUB)),
            (shape((poles, features), F32), cols(poles)),
        ],
        [
            pltpu.VMEM((2 * SUB, WIDE), BF16),
            pltpu.VMEM((2 * SUB - STRIP, WIDE), BF16),
            pltpu.VMEM((SUB, WIDE), F32),
        ],
        "early",
        4 * SUB * SUB * features * 8,
        (gate_in, values, gate_mid, medium_taps, rate_rows, residue_rows, med_skip, lng_skip),
    )
    gated, first, total, message = call(
        functools.partial(late_kernel, per_group, poles),
        steps,
        [cols(SUB), cols(SUB), cols(SUB), cols(SUB), cols(SUB), tall(strip_rows, MED + STRIP),
         tall(WIDE // per_group * poles, SUB), cols(poles), cols(1), cols(poles)],
        [
            (shape((SUB, features), BF16), cols(SUB)),
            (shape((poles, features), F32), cols(poles)),
            (shape((poles, features), F32), cols(poles)),
            (shape((poles, features), BF16), cols(poles)),
        ],
        [pltpu.VMEM((2 * SUB, WIDE), BF16), pltpu.VMEM((SUB, WIDE), F32)],
        "late",
        2 * SUB * SUB * features * 8,
        (halo_a, halo_b, gate_in, values, gate_mid, med_strips, folds, rates_pc, med_skip, later),
    )
    part_a, lift = call(
        functools.partial(inner_kernel, per_group, poles),
        steps,
        [cols(SUB), tall(strip_rows, SUB), table, table, cols(1)],
        [(shape((SUB, features), F32), cols(SUB)), (shape((SUB, features), BF16), cols(SUB))],
        [pltpu.VMEM((2 * SUB - STRIP, WIDE), BF16)],
        "inner",
        2 * SUB * SUB * features * 8,
        (gated, long_strips, rate_rows, residue_rows, lng_skip),
    )
    carry = scan_states(total, message, rates_pc, row_count)
    (mixed,) = call(
        functools.partial(final_kernel, per_group, poles),
        steps,
        [cols(poles), cols(poles), cols(poles), cols(SUB), cols(SUB), cols(SUB), cols(row_count)],
        [(shape((row_count, features), BF16), cols(row_count))],
        [],
        "final",
        2 * SUB * SUB * features * 2,
        (carry, first, rates_pc, lift, part_a, part_b, gate_out),
    )
    return mixed


def solution(mesh):
    rows = P(("grp", "seq"), None)
    return jax.shard_map(
        shards,
        mesh=mesh,
        in_specs=(rows,) * 4 + (P(),) * 5,
        out_specs=rows,
        check_vma=False,
    )
```

time: 359 us -> 87.1 us (0.24)
  local copies, waits for them, and re-layouts: 278 us -> 9.54 us
  Pallas kernels: 0 us -> 49.1 us
  matrix products: 36.7 us -> 0 us
  other arithmetic: 26.3 us -> 4.22 us
  waiting for transfers between devices: 0.2 us -> 9.23 us
    reshape x11 -> x2, local copies, waits for them, and re-layouts: 153 us -> 0.2 us  [the longest x1 0.1 us: shards(): residue_rows = residues.reshape(-1, LANES)]
    unnamed x42, local copies, waits for them, and re-layouts: 64.7 us -> 9.34 us
    pallas_call x0 -> x4, Pallas kernels: none -> 49.1 us  [call(): pl.pallas_call(kernel, grid=(grid,), in_specs=in_specs, out_specs=[spec f...]
    dot_general x5 -> x0, matrix products: 36.7 us -> none  [the longest x1 11.3 us: shards(): jnp.einsum('lkw,lyw->lyk', middle_filter_matrix, sliding_spans, preferred...]
    slice x20 -> x0, local copies, waits for them, and re-layouts: 32.3 us -> none  [the longest x2 27.1 us: banded(): tiled = jnp.tile(cycle, (1, out_rows))[:, :out_rows * (period - 1)]]
    all_to_all x2 -> x0, starting transfers between devices: 12.3 us -> none  [the longest x1 6.24 us: shards(): lax.all_to_all(flat_states, 'seq', split_axis=1, concat_axis=0, tiled=True)]
    ppermute x1 -> x7, starting transfers between devices: 3.35 us -> 13.8 us  [the longest x5 9.64 us: swap(): return lax.ppermute(value, 'seq', route)]
    ppermute x1 -> x7, waiting for transfers between devices: 0.01 us -> 9.23 us  [the longest x5 9.22 us: swap(): return lax.ppermute(value, 'seq', route)]
  transfers between devices with their start and end apart: 3 -> 7, of which waited for: 1 -> 4; matrix products, arithmetic and copies ran while one was open for 68% -> 1% of each run, Pallas kernels for 0% -> 33%
where the time goes in v1:
time: 87.1 us; the launch traced here: 86 us
  Pallas kernels  49.1 us (56%)
  starting transfers between devices  13.8 us (16%)
  local copies, waits for them, and re-layouts  9.54 us (11%)
  waiting for transfers between devices  9.23 us (11%)
  other arithmetic  4.22 us (5%)
    pallas_call x4, Pallas kernels, call(): pl.pallas_call(kernel, grid=(grid,), in_specs=in_specs, out_specs=[spec f...  49.1 us
    ppermute x5, starting transfers between devices, swap(): return lax.ppermute(value, 'seq', route)  9.64 us
    unnamed x42, local copies, waits for them, and re-layouts  9.34 us
    ppermute x5, waiting for transfers between devices, swap(): return lax.ppermute(value, 'seq', route)  9.22 us
    convert_element_type x1, other arithmetic, shards(): (gate_in[row_count - SUB:].astype(F32) * values[row_count - SUB:].astype(...  2.9 us
    ppermute x1, starting transfers between devices, shards(): lax.ppermute(tail, 'seq', [(i, i + 1) for i in range(0, count - 1, 2)])  2.46 us
  transfers between devices with their start and end apart: 7, of which 4 were waited for; matrix products, arithmetic and copies ran while one was open for 1% of the time, Pallas kernels for 33%

profile of v1, /device:TPU:0, one launch (start us, length us, event | category | flops | bytes accessed | tf_op | source)
XLA Modules:
  0.0 86.0 jit_solution(8846990250023678729)
XLA Ops:
  0.0 2.9 %multiply_convert_fusion = bf16[128,4096]{1,0:T(8,128)(2,1)} fusion(bf16[256,4096]{1,0:T(8,128)(2,1)} %values.3, bf16[256,4096]{1,0:T(8,128)(2,1)} %gate_in.3), kind=kLoop, calls=%fused_computation | loop fusion | flops 2097152 | bytes 3145728 | tf_op jit(solution)/shard_map/convert_element_type | solution.py:254
  2.9 2.5 %collective-permute-start = (bf16[128,4096]{1,0:T(8,128)(2,1)}, bf16[128,4096]{1,0:T(8,128)(2,1)S(1)}, u32[]{:S(2)}, u32[]{:S(2)}) collective-permute-start(bf16[128,4096]{1,0:T(8,128)(2,1)} %multiply_convert_fusion), channel_id=1, source_target_pairs={{0,1},{2,3},{4,5},{6,7},{8,9},{10,11},{12,13},{14,15},{16,17},{18,... | collective-permute-start | bytes 3145736 | tf_op jit(solution)/shard_map/ppermute | solution.py:258
  5.4 1.7 %collective-permute-start.1 = (bf16[128,4096]{1,0:T(8,128)(2,1)}, bf16[128,4096]{1,0:T(8,128)(2,1)}, u32[]{:S(2)}, u32[]{:S(2)}) collective-permute-start(bf16[128,4096]{1,0:T(8,128)(2,1)} %multiply_convert_fusion), channel_id=1, source_target_pairs={{1,2},{3,4},{5,6},{7,8},{9,10},{11,12},{13,14},{17,18},{19,20},{21... | collective-permute-start | bytes 3145736 | tf_op jit(solution)/shard_map/ppermute | solution.py:257
  7.1 0.1 copy.12
  7.2 0.1 reshape.6.rates
  7.3 0.1 copy.13
  7.4 0.1 reshape.7.residues
  7.5 1.6 %copy-done.1 = bf16[256,4096]{1,0:T(8,128)(2,1)S(1)} copy-done((bf16[256,4096]{1,0:T(8,128)(2,1)S(1)}, bf16[256,4096]{1,0:T(8,128)(2,1)}, u32[]{:S(2)}) %copy-start.1) | copy-done | bytes 2097176
  9.1 1.6 %copy-done.5 = bf16[256,4096]{1,0:T(8,128)(2,1)S(1)} copy-done((bf16[256,4096]{1,0:T(8,128)(2,1)S(1)}, bf16[256,4096]{1,0:T(8,128)(2,1)}, u32[]{:S(2)}) %copy-start.5) | copy-done | bytes 2097176
  10.7 23.0 %early.1 = (bf16[8192,160]{1,0:T(8,128)(2,1)S(1)}, bf16[8192,128]{1,0:T(8,128)(2,1)S(1)}, bf16[4096,128]{1,0:T(8,128)(2,1)S(1)}, f32[16,4096]{1,0:T(8,128)S(1)},...) custom-call(bf16[256,4096]{1,0:T(8,128)(2,1)S(1)} %copy-done.1, bf16[256,4096]{1,0:T(8,128)(2,1)S(1)} %copy-done, ...), custom_call_target="tpu_custom_call" | custom-call | flops 2147483648 | bytes 14811136 | tf_op jit(solution)/shard_map/early/pallas_call | solution.py:191
  33.7 1.3 %copy-done.14 = bf16[8192,128]{1,0:T(8,128)(2,1)} copy-done((bf16[8192,128]{1,0:T(8,128)(2,1)}, bf16[8192,128]{1,0:T(8,128)(2,1)S(1)}, u32[]{:S(2)}) %copy-start.14) | copy-done | bytes 2097176
  35.1 13.3 %late.1 = (bf16[128,4096]{1,0:T(8,128)(2,1)S(1)}, f32[16,4096]{1,0:T(8,128)S(1)}, f32[16,4096]{1,0:T(8,128)S(1)}, bf16[16,4096]{1,0:T(8,128)(2,1)}) custom-call(bf16[128,4096]{1,0:T(8,128)(2,1)S(1)} %collective-permute-done.halo_a, bf16[128,4096]{1,0:T(8,128)(2,1)} %collective-permute-done.1.halo_b, bf16[256,4096]{1,0:T(8,128)(2,1)S(1)} %copy-done.1, ...), custom_call_target="tpu_custom_call" | custom-call | flops 1073741824 | bytes 14303232 | tf_op jit(solution)/shard_map/late/pallas_call | solution.py:191
  48.3 0.7 copy-done.6
  49.0 0.7 copy-done.8
  49.8 1.0 %copy-done.10 = bf16[128,4096]{1,0:T(8,128)(2,1)} copy-done((bf16[128,4096]{1,0:T(8,128)(2,1)}, bf16[128,4096]{1,0:T(8,128)(2,1)S(1)}, u32[]{:S(2)}) %copy-start.10) | copy-done | bytes 1048600
  50.7 3.7 %collective-permute-start.2 = (bf16[16,4096]{1,0:T(8,128)(2,1)}, bf16[16,4096]{1,0:T(8,128)(2,1)S(1)}, u32[]{:S(2)}, u32[]{:S(2)}) collective-permute-start(bf16[16,4096]{1,0:T(8,128)(2,1)} %get-tuple-element.21), channel_id=1, source_target_pairs={{0,1},{1,0},{2,3},{3,2},{4,5},{5,4},{6,7},{7,6},{8,9},{9,8},{10,11... | collective-permute-start | bytes 393224 | tf_op jit(solution)/shard_map/ppermute | solution.py:209
  54.5 1.1 %collective-permute-done.2 = bf16[16,4096]{1,0:T(8,128)(2,1)S(1)} collective-permute-done((bf16[16,4096]{1,0:T(8,128)(2,1)}, bf16[16,4096]{1,0:T(8,128)(2,1)S(1)}, u32[]{:S(2)}, u32[]{:S(2)}) %collective-permute-start.2) | collective-permute-done | bytes 131104 | tf_op jit(solution)/shard_map/ppermute | solution.py:209
  55.6 0.6 copy-done.16
  56.3 0.9 %fusion.13 = (bf16[16,2048]{1,0:T(8,128)(2,1)S(1)}, f32[16,2048]{1,0:T(8,128)S(1)}) fusion(f32[16,4096]{1,0:T(8,128)} %copy-done.8, s32[]{:T(128)S(6)} %select_n.126, f32[16,4096]{1,0:T(8,128)S(1)} %convert_element_type.49, pred[]{:T(512)S(6)} %eq.20, f32[16,4096]{1,0:T(8,128)S(1)} %multiply_exponential_fusion), kind=kLoop, calls=%fused_computation.27 | loop fusion | flops 163840 | bytes 589829 | tf_op jit(solution)/shard_map/convert_element_type | solution.py:227
  57.2 1.6 %collective-permute-start.3 = (bf16[16,2048]{1,0:T(8,128)(2,1)S(1)}, bf16[16,2048]{1,0:T(8,128)(2,1)S(1)}, u32[]{:S(2)}, u32[]{:S(2)}) collective-permute-start(bf16[16,2048]{1,0:T(8,128)(2,1)S(1)} %get-tuple-element.29), channel_id=1, source_target_pairs={{0,2},{1,3},{2,0},{3,1},{4,6},{5,7},{6,4},{7,5},{8,10},{9,11},{10,... | collective-permute-start | bytes 196616 | tf_op jit(solution)/shard_map/ppermute | solution.py:209
  58.8 2.8 %collective-permute-done.3 = bf16[16,2048]{1,0:T(8,128)(2,1)S(1)} collective-permute-done((bf16[16,2048]{1,0:T(8,128)(2,1)S(1)}, bf16[16,2048]{1,0:T(8,128)(2,1)S(1)}, u32[]{:S(2)}, u32[]{:S(2)}) %collective-permute-start.3) | collective-permute-done | bytes 65568 | tf_op jit(solution)/shard_map/ppermute | solution.py:209
  61.7 1.6 %collective-permute-start.4 = (bf16[16,2048]{1,0:T(8,128)(2,1)S(1)}, bf16[16,2048]{1,0:T(8,128)(2,1)S(1)}, u32[]{:S(2)}, u32[]{:S(2)}) collective-permute-start(bf16[16,2048]{1,0:T(8,128)(2,1)S(1)} %fusion.12), channel_id=1, source_target_pairs={{0,4},{1,5},{2,6},{3,7},{4,0},{5,1},{6,2},{7,3},{8,12},{9,13},{10,... | collective-permute-start | bytes 196616 | tf_op jit(solution)/shard_map/ppermute | solution.py:209
  63.3 2.7 %collective-permute-done.4 = bf16[16,2048]{1,0:T(8,128)(2,1)S(1)} collective-permute-done((bf16[16,2048]{1,0:T(8,128)(2,1)S(1)}, bf16[16,2048]{1,0:T(8,128)(2,1)S(1)}, u32[]{:S(2)}, u32[]{:S(2)}) %collective-permute-start.4) | collective-permute-done | bytes 65568 | tf_op jit(solution)/shard_map/ppermute | solution.py:209
  66.0 0.1 fusion.10
  66.1 2.6 %collective-permute-start.5 = (bf16[16,2048]{1,0:T(8,128)(2,1)S(1)}, bf16[16,2048]{1,0:T(8,128)(2,1)S(1)}, u32[]{:S(2)}, u32[]{:S(2)}) collective-permute-start(bf16[16,2048]{1,0:T(8,128)(2,1)S(1)} %fusion.10), channel_id=1, source_target_pairs={{0,8},{1,9},{2,10},{3,11},{4,12},{5,13},{6,14},{7,15},{8,0},{9,1},... | collective-permute-start | bytes 196616 | tf_op jit(solution)/shard_map/ppermute | solution.py:209
  68.7 2.6 %collective-permute-done.5 = bf16[16,2048]{1,0:T(8,128)(2,1)S(1)} collective-permute-done((bf16[16,2048]{1,0:T(8,128)(2,1)S(1)}, bf16[16,2048]{1,0:T(8,128)(2,1)S(1)}, u32[]{:S(2)}, u32[]{:S(2)}) %collective-permute-start.5) | collective-permute-done | bytes 65568 | tf_op jit(solution)/shard_map/ppermute | solution.py:209
  71.3 0.1 fusion.4
  71.4 0.1 collective-permute-start.6
  71.5 1.6 %copy-done.15 = bf16[8192,128]{1,0:T(8,128)(2,1)S(1)} copy-done((bf16[8192,128]{1,0:T(8,128)(2,1)S(1)}, bf16[8192,128]{1,0:T(8,128)(2,1)}, u32[]{:S(2)}) %copy-start.15) | copy-done | bytes 2097176
  73.1 5.3 %inner.1 = (f32[128,4096]{1,0:T(8,128)S(1)}, bf16[128,4096]{1,0:T(8,128)(2,1)S(1)}) custom-call(bf16[128,4096]{1,0:T(8,128)(2,1)S(1)} %copy-done.11, bf16[8192,128]{1,0:T(8,128)(2,1)S(1)} %copy-done.15, f32[32,128]{1,0:T(8,128)S(1)} %reshape.6.rates, f32[32,128]{1,0:T(8,128)S(1)} %reshape.7.residues, f32[1,4096]{1,0:T(1,128)S(1)} %bitcast.5), custom_call_target="tpu_custom_call" | custom-call | flops 1073741824 | bytes 6340608 | tf_op jit(solution)/shard_map/inner/pallas_call | solution.py:191
  78.4 0.1 convert_select_fusion.carry
  78.6 7.5 %final.1 = bf16[256,4096]{1,0:T(8,128)(2,1)} custom-call(f32[16,4096]{1,0:T(8,128)S(1)} %convert_select_fusion.carry, f32[16,4096]{1,0:T(8,128)S(1)} %copy-done.7, f32[16,4096]{1,0:T(8,128)S(1)} %get-tuple-element.17.rates_pc, bf16[128,4096]{1,0:T(8,128)(2,1)S(1)} %get-tuple-element.26.lift, f32[128,4096]{1,0:T(8,128)S(1)} %get-tuple-element.27.part_a, ...), custom_call_target="tpu_custom_call" | custom-call | flops 268435456 | bytes 10223616 | tf_op jit(solution)/shard_map/final/pallas_call | solution.py:191
  (39 shorter events, 0.2 us)
Async XLA Ops:
  0.0 7.5 %copy-start = (bf16[256,4096]{1,0:T(8,128)(2,1)S(1)}, bf16[256,4096]{1,0:T(8,128)(2,1)}, u32[]{:S(2)}) copy-start(bf16[256,4096]{1,0:T(8,128)(2,1)} %values.3) | copy-start | bytes 6291460
  0.0 7.1 %copy-start.18 = (f32[256,16]{0,1:T(8,128)S(1)}, f32[256,16]{0,1:T(8,128)}, u32[]{:S(2)}) copy-start(f32[256,16]{0,1:T(8,128)} %param.16) | copy-start | bytes 49156
  0.0 7.3 %copy-start.19 = (f32[256,16]{0,1:T(8,128)S(1)}, f32[256,16]{0,1:T(8,128)}, u32[]{:S(2)}) copy-start(f32[256,16]{0,1:T(8,128)} %param.15) | copy-start | bytes 49156
  0.0 7.5 %copy-start.12 = (bf16[256,128]{1,0:T(8,128)(2,1)S(1)}, bf16[256,128]{1,0:T(8,128)(2,1)}, u32[]{:S(2)}) copy-start(bf16[256,128]{1,0:T(8,128)(2,1)} %taps.1) | copy-start | bytes 196612
  0.0 7.5 %copy-start.9 = (f32[4096]{0:T(1024)S(1)}, f32[4096]{0:T(1024)}, u32[]{:S(2)}) copy-start(f32[4096]{0:T(1024)} %param.14) | copy-start | bytes 49156
  0.0 7.5 %copy-start.13 = (f32[4096]{0:T(1024)S(1)}, f32[4096]{0:T(1024)}, u32[]{:S(2)}) copy-start(f32[4096]{0:T(1024)} %param.17) | copy-start | bytes 49156
  2.9 32.1 %collective-permute-start = (bf16[128,4096]{1,0:T(8,128)(2,1)}, bf16[128,4096]{1,0:T(8,128)(2,1)S(1)}, u32[]{:S(2)}, u32[]{:S(2)}) collective-permute-start(bf16[128,4096]{1,0:T(8,128)(2,1)} %multiply_convert_fusion), channel_id=1, source_target_pairs={{0,1},{2,3},{4,5},{6,7},{8,9},{10,11},{12,13},{14,15},{16,17},{18,... | collective-permute-start | bytes 3145736 | tf_op jit(solution)/shard_map/ppermute | solution.py:258
  5.4 29.7 %collective-permute-start.1 = (bf16[128,4096]{1,0:T(8,128)(2,1)}, bf16[128,4096]{1,0:T(8,128)(2,1)}, u32[]{:S(2)}, u32[]{:S(2)}) collective-permute-start(bf16[128,4096]{1,0:T(8,128)(2,1)} %multiply_convert_fusion), channel_id=1, source_target_pairs={{1,2},{3,4},{5,6},{7,8},{9,10},{11,12},{13,14},{17,18},{19,20},{21... | collective-permute-start | bytes 3145736 | tf_op jit(solution)/shard_map/ppermute | solution.py:257
  7.5 1.6 %copy-start.1 = (bf16[256,4096]{1,0:T(8,128)(2,1)S(1)}, bf16[256,4096]{1,0:T(8,128)(2,1)}, u32[]{:S(2)}) copy-start(bf16[256,4096]{1,0:T(8,128)(2,1)} %gate_in.3) | copy-start | bytes 6291460
  9.1 1.6 %copy-start.5 = (bf16[256,4096]{1,0:T(8,128)(2,1)S(1)}, bf16[256,4096]{1,0:T(8,128)(2,1)}, u32[]{:S(2)}) copy-start(bf16[256,4096]{1,0:T(8,128)(2,1)} %gate_mid.3) | copy-start | bytes 6291460
  33.7 1.3 %copy-start.14 = (bf16[8192,128]{1,0:T(8,128)(2,1)}, bf16[8192,128]{1,0:T(8,128)(2,1)S(1)}, u32[]{:S(2)}) copy-start(bf16[8192,128]{1,0:T(8,128)(2,1)S(1)} %get-tuple-element.25.long_strips) | copy-start | bytes 6291460
  35.0 13.3 %copy-start.3 = (f32[128,4096]{1,0:T(8,128)}, f32[128,4096]{1,0:T(8,128)S(1)}, u32[]{:S(2)}) copy-start(f32[128,4096]{1,0:T(8,128)S(1)} %get-tuple-element.28.part_b) | copy-start | bytes 6291460
  48.3 0.7 copy-start.6
  49.0 0.7 copy-start.8
  49.8 1.0 %copy-start.10 = (bf16[128,4096]{1,0:T(8,128)(2,1)}, bf16[128,4096]{1,0:T(8,128)(2,1)S(1)}, u32[]{:S(2)}) copy-start(bf16[128,4096]{1,0:T(8,128)(2,1)S(1)} %get-tuple-element.24.gated) | copy-start | bytes 3145732
  50.7 20.8 %copy-start.11 = (bf16[128,4096]{1,0:T(8,128)(2,1)S(1)}, bf16[128,4096]{1,0:T(8,128)(2,1)}, u32[]{:S(2)}) copy-start(bf16[128,4096]{1,0:T(8,128)(2,1)} %copy-done.10) | copy-start | bytes 3145732
  50.7 4.9 %collective-permute-start.2 = (bf16[16,4096]{1,0:T(8,128)(2,1)}, bf16[16,4096]{1,0:T(8,128)(2,1)S(1)}, u32[]{:S(2)}, u32[]{:S(2)}) collective-permute-start(bf16[16,4096]{1,0:T(8,128)(2,1)} %get-tuple-element.21), channel_id=1, source_target_pairs={{0,1},{1,0},{2,3},{3,2},{4,5},{5,4},{6,7},{7,6},{8,9},{9,8},{10,11... | collective-permute-start | bytes 393224 | tf_op jit(solution)/shard_map/ppermute | solution.py:209
  55.6 0.6 copy-start.16
  57.2 4.4 %collective-permute-start.3 = (bf16[16,2048]{1,0:T(8,128)(2,1)S(1)}, bf16[16,2048]{1,0:T(8,128)(2,1)S(1)}, u32[]{:S(2)}, u32[]{:S(2)}) collective-permute-start(bf16[16,2048]{1,0:T(8,128)(2,1)S(1)} %get-tuple-element.29), channel_id=1, source_target_pairs={{0,2},{1,3},{2,0},{3,1},{4,6},{5,7},{6,4},{7,5},{8,10},{9,11},{10,... | collective-permute-start | bytes 196616 | tf_op jit(solution)/shard_map/ppermute | solution.py:209
  61.7 4.3 %collective-permute-start.4 = (bf16[16,2048]{1,0:T(8,128)(2,1)S(1)}, bf16[16,2048]{1,0:T(8,128)(2,1)S(1)}, u32[]{:S(2)}, u32[]{:S(2)}) collective-permute-start(bf16[16,2048]{1,0:T(8,128)(2,1)S(1)} %fusion.12), channel_id=1, source_target_pairs={{0,4},{1,5},{2,6},{3,7},{4,0},{5,1},{6,2},{7,3},{8,12},{9,13},{10,... | collective-permute-start | bytes 196616 | tf_op jit(solution)/shard_map/ppermute | solution.py:209
  66.1 5.2 %collective-permute-start.5 = (bf16[16,2048]{1,0:T(8,128)(2,1)S(1)}, bf16[16,2048]{1,0:T(8,128)(2,1)S(1)}, u32[]{:S(2)}, u32[]{:S(2)}) collective-permute-start(bf16[16,2048]{1,0:T(8,128)(2,1)S(1)} %fusion.10), channel_id=1, source_target_pairs={{0,8},{1,9},{2,10},{3,11},{4,12},{5,13},{6,14},{7,15},{8,0},{9,1},... | collective-permute-start | bytes 196616 | tf_op jit(solution)/shard_map/ppermute | solution.py:209
  71.3 7.1 %copy-start.17 = (bf16[16,4096]{1,0:T(8,128)(2,1)S(1)}, bf16[16,4096]{1,0:T(8,128)(2,1)}, u32[]{:S(2)}) copy-start(bf16[16,4096]{1,0:T(8,128)(2,1)} %copy-done.16) | copy-start | bytes 393220
  71.4 7.0 %collective-permute-start.6 = (bf16[16,2048]{1,0:T(8,128)(2,1)S(1)}, bf16[16,2048]{1,0:T(8,128)(2,1)S(1)}, u32[]{:S(2)}, u32[]{:S(2)}) collective-permute-start(bf16[16,2048]{1,0:T(8,128)(2,1)S(1)} %fusion.4), channel_id=1, source_target_pairs={{0,1},{1,0},{2,3},{3,2},{4,5},{5,4},{6,7},{7,6},{8,9},{9,8},{10,11... | collective-permute-start | bytes 196616 | tf_op jit(solution)/shard_map/ppermute | solution.py:209
  71.5 1.6 %copy-start.15 = (bf16[8192,128]{1,0:T(8,128)(2,1)S(1)}, bf16[8192,128]{1,0:T(8,128)(2,1)}, u32[]{:S(2)}) copy-start(bf16[8192,128]{1,0:T(8,128)(2,1)} %copy-done.14) | copy-start | bytes 6291460
  73.1 5.4 %copy-start.2 = (bf16[256,4096]{1,0:T(8,128)(2,1)S(1)}, bf16[256,4096]{1,0:T(8,128)(2,1)}, u32[]{:S(2)}) copy-start(bf16[256,4096]{1,0:T(8,128)(2,1)} %gate_out.1) | copy-start | bytes 6291460
  73.1 5.4 %copy-start.4 = (f32[128,4096]{1,0:T(8,128)S(1)}, f32[128,4096]{1,0:T(8,128)}, u32[]{:S(2)}) copy-start(f32[128,4096]{1,0:T(8,128)} %copy-done.3) | copy-start | bytes 6291460
  73.1 5.4 %copy-start.7 = (f32[16,4096]{1,0:T(8,128)S(1)}, f32[16,4096]{1,0:T(8,128)}, u32[]{:S(2)}) copy-start(f32[16,4096]{1,0:T(8,128)} %copy-done.6) | copy-start | bytes 786436

commit v2 on v1

v2 whole, which is shorter than its diff:
```python
import functools

import jax
import jax.numpy as jnp
from jax import lax
from jax.experimental import pallas as pl
from jax.experimental.pallas import tpu as pltpu
from jax.sharding import PartitionSpec as P

MED = 128
SUB = 128
STRIP = 32
LANES = 128
WIDE = 1024
CHUNK = 1024
PIECES = 4
BF16 = jnp.bfloat16
F32 = jnp.float32


def dot(a, b, precision=None):
    return jnp.dot(a, b, preferred_element_type=F32, precision=precision)


def own_groups(stack, rows, per_group):
    groups = stack.shape[0] // rows
    owner = lax.broadcasted_iota(jnp.int32, (rows, stack.shape[1]), 1) % LANES // per_group
    kept = stack[:rows]
    for g in range(1, groups):
        kept = jnp.where(owner == g, stack[g * rows : (g + 1) * rows], kept)
    return kept


def toeplitz(line, g):
    spread = jnp.broadcast_to(line[g : g + 1], (STRIP, 2 * LANES))
    return pltpu.roll(spread, 0, 1, stride=1, stride_axis=0)


def pair_of_strips(window, start, depth, lanes):
    return jnp.concatenate(
        [window[start : start + depth, lanes], window[start + STRIP : start + STRIP + depth, lanes]],
        axis=1,
    )


def medium_block(strips, window, lanes, per_group):
    rows = []
    for i in range(0, SUB // STRIP, 2):
        both = own_groups(
            dot(strips, pair_of_strips(window, i * STRIP, MED + STRIP, lanes)), STRIP, per_group
        )
        rows += [both[:, :LANES], both[:, LANES:]]
    return jnp.concatenate(rows, axis=0)


def inner_block(strips, window, lanes, per_group):
    rows = []
    for i in range(0, SUB // STRIP, 2):
        both = own_groups(
            dot(strips, pair_of_strips(window, i * STRIP, SUB, lanes)), STRIP, per_group
        )
        rows += [both[:, :LANES], both[:, LANES:]]
    return jnp.concatenate(rows, axis=0)


def lanes_at(step, b):
    return pl.ds(pl.multiple_of(step * WIDE + b * LANES, LANES), LANES)


def rows_at(step, b, rows_per_block):
    start = (step * (WIDE // LANES) + b) * rows_per_block
    return pl.ds(pl.multiple_of(start, rows_per_block), rows_per_block)


def early_kernel(
    per_group, poles,
    gate_in, values, gate_mid, taps, rates, med_skip,
    med_strips, folds, rates_pc, product, mid_first, gated_out, state,
    in_buf, value_buf, mid_buf, line, window, sems,
):
    features = gate_in.shape[1]
    block = LANES // per_group
    copies = []
    for c in range(features // CHUNK):
        lanes = pl.ds(c * CHUNK, CHUNK)
        copies.append(
            [
                pltpu.make_async_copy(gate_in.at[:, lanes], in_buf.at[:, lanes], sems.at[c, 0]),
                pltpu.make_async_copy(values.at[:, lanes], value_buf.at[:, lanes], sems.at[c, 1]),
                pltpu.make_async_copy(
                    gate_mid.at[pl.ds(SUB, SUB), lanes], mid_buf.at[:, lanes], sems.at[c, 2]
                ),
                pltpu.make_async_copy(
                    gate_mid.at[pl.ds(0, SUB), lanes], mid_first.at[:, lanes], sems.at[c, 3]
                ),
            ]
        )
        for copy in copies[-1]:
            copy.start()
    tap = lax.broadcasted_iota(jnp.int32, (LANES, 2 * LANES), 0)
    spot = lax.broadcasted_iota(jnp.int32, (LANES, 2 * LANES), 1)
    line[...] = dot(taps[...], (spot == MED - tap).astype(BF16))
    offset = lax.broadcasted_iota(jnp.int32, (LANES, LANES), 1).astype(F32)

    def one(step):
        for b in range(WIDE // LANES):
            at = lanes_at(step, b)
            here = slice(b * LANES, (b + 1) * LANES)
            rate_row = rates[pl.ds(step * (WIDE // LANES) + b, 1), :]
            rate_col = jnp.transpose(jnp.broadcast_to(rate_row, (LANES, LANES)))
            rates_pc[:, at] = own_groups(rate_col, poles, per_group)
            fold = jnp.exp(-rate_col * (SUB - 1.0 - offset)).astype(BF16)
            folds[rows_at(step, b, LANES), :] = fold
            first = (step * (WIDE // LANES) + b) * block
            lines = line[pl.ds(pl.multiple_of(first, block), block), :]
            strips = jnp.concatenate(
                [toeplitz(lines, g)[:, : MED + STRIP].astype(BF16) for g in range(block)], axis=0
            )
            med_strips[rows_at(step, b, block * STRIP), :] = strips
            rows = (in_buf[:, at].astype(F32) * value_buf[:, at].astype(F32)).astype(BF16)
            window[:, here] = rows
            product[:, at] = rows[:SUB]
            medium = medium_block(strips, window, here, per_group)
            medium = medium + med_skip[:, at] * rows[SUB:].astype(F32)
            gated = (mid_buf[:, at].astype(F32) * medium).astype(BF16)
            gated_out[:, at] = gated
            state[:, at] = own_groups(dot(fold, gated), poles, per_group)

    for c in range(features // CHUNK):
        for copy in copies[c]:
            copy.wait()
        pl.loop(c * (CHUNK // WIDE), (c + 1) * (CHUNK // WIDE))(one)


def late_kernel(
    per_group, poles,
    halo, product, gate_mid, med_strips, folds, rates_pc, med_skip, later,
    gated_out, state, total, message,
    window,
):
    features = product.shape[1]
    block = LANES // per_group
    def one(step):
        for b in range(WIDE // LANES):
            at = lanes_at(step, b)
            here = slice(b * LANES, (b + 1) * LANES)
            rows = product[:, at]
            window[:SUB, here] = halo[:, at]
            window[SUB:, here] = rows
            strips = med_strips[rows_at(step, b, block * STRIP), :]
            medium = medium_block(strips, window, here, per_group)
            medium = medium + med_skip[:, at] * rows.astype(F32)
            gated = (gate_mid[:, at].astype(F32) * medium).astype(BF16)
            gated_out[:, at] = gated
            fold = folds[rows_at(step, b, LANES), :]
            first = own_groups(dot(fold, gated), poles, per_group)
            state[:, at] = first
            whole = jnp.exp(-rates_pc[:, at] * SUB) * first + later[:, at]
            total[:, at] = whole
            message[:, at] = whole.astype(BF16)

    pl.loop(0, features // WIDE)(one)


def column(row):
    return jnp.transpose(jnp.broadcast_to(row, (LANES, LANES)))


def inner_kernel(
    per_group, poles, base,
    gated_a, gated_b, rates, residues, long_skip, gate_out,
    part, lift, gate_copy, token,
    taps, line, padded, sem,
):
    width = part.shape[1]
    block = LANES // per_group
    copy = pltpu.make_async_copy(gate_out.at[:, pl.ds(base, width)], gate_copy, sem)
    copy.start()
    offset = lax.broadcasted_iota(jnp.int32, (LANES, LANES), 1).astype(F32)
    after = lax.broadcasted_iota(jnp.int32, (SUB, LANES), 0).astype(F32) + 1.0
    for k in range(2):
        padded[k, : SUB - STRIP] = jnp.zeros((SUB - STRIP, WIDE), BF16)
    for b in range(width // LANES):
        row = slice(base // LANES + b, base // LANES + b + 1)
        rate_row = rates[row, :]
        residue_row = residues[row, :]
        here = slice(b * LANES, (b + 1) * LANES)
        lift[:, here] = (residue_row * jnp.exp(-rate_row * after)).astype(BF16)
        terms = column(residue_row) * jnp.exp(-column(rate_row) * offset)
        taps[b * block : (b + 1) * block, :] = jnp.sum(
            terms.reshape(block, poles, LANES), axis=1
        ).astype(BF16)
    tap = lax.broadcasted_iota(jnp.int32, (LANES, 2 * LANES), 0)
    spot = lax.broadcasted_iota(jnp.int32, (LANES, 2 * LANES), 1)
    turn = (spot == (SUB - STRIP - tap + 2 * LANES) % (2 * LANES)).astype(BF16)
    line[...] = dot(taps[...], turn)

    @pl.loop(0, width // WIDE)
    def _(step):
        for b in range(WIDE // LANES):
            at = lanes_at(step, b)
            source = pl.ds(pl.multiple_of(base + step * WIDE + b * LANES, LANES), LANES)
            here = slice(b * LANES, (b + 1) * LANES)
            lines = line[rows_at(step, b, block), :]
            strips = jnp.concatenate(
                [toeplitz(lines, g)[:, :LANES].astype(BF16) for g in range(block)], axis=0
            )
            for k, gated in enumerate((gated_a, gated_b)):
                rows = gated[:, source]
                padded[k, SUB - STRIP :, here] = rows
                part[k * SUB : (k + 1) * SUB, at] = inner_block(
                    strips, padded.at[k], here, per_group
                ) + long_skip[:, source] * rows.astype(F32)

    token[...] = part[:1, :LANES]
    copy.wait()


def spread_groups(state, per_group, poles):
    tall = jnp.concatenate([state] * (LANES // per_group), axis=0)
    owner = lax.broadcasted_iota(jnp.int32, tall.shape, 1) // per_group
    mine = lax.broadcasted_iota(jnp.int32, tall.shape, 0) // poles
    return jnp.where(owner == mine, tall, 0.0).astype(BF16)


def final_kernel(per_group, poles, own, other, partner, state, rates_pc, *refs):
    parts, lifts, gates = (refs[k * PIECES : (k + 1) * PIECES] for k in range(3))
    mixed, out, sems = refs[3 * PIECES :]
    width = parts[0].shape[1]
    half = own.shape[1]
    positions = mixed.shape[0]
    upper = lax.axis_index("seq") % 2
    copies = []
    for piece, (part, lift, gate) in enumerate(zip(parts, lifts, gates)):

        @pl.loop(0, width // WIDE)
        def _(step):
            for b in range(WIDE // LANES):
                at = lanes_at(step, b)
                to = pl.ds(pl.multiple_of(piece * width + step * WIDE + b * LANES, LANES), LANES)
                side = piece * width // half
                inside = piece * width - side * half + step * WIDE + b * LANES
                inside = pl.ds(pl.multiple_of(inside, LANES), LANES)
                rate = rates_pc[:, to]
                start = jnp.where(upper == side, own[:, inside], other[:, inside].astype(F32))
                device = jnp.exp(-rate * positions) * start + partner[:, to].astype(F32)
                start = jnp.where(upper == 1, device, start)
                middle = jnp.exp(-rate * SUB) * start + state[:, to]
                before = jnp.concatenate(
                    [spread_groups(start, per_group, poles), spread_groups(middle, per_group, poles)],
                    axis=1,
                )
                lifted = dot(lift[:, at], before)
                for k in range(2):
                    rows = slice(k * SUB, (k + 1) * SUB)
                    long_out = part[rows, at] + lifted[:, k * LANES : (k + 1) * LANES]
                    out[rows, to] = (gate[rows, at].astype(F32) * long_out).astype(BF16)

        lanes = pl.ds(piece * width, width)
        copies.append(pltpu.make_async_copy(out.at[:, lanes], mixed.at[:, lanes], sems.at[piece]))
        copies[-1].start()
    for copy in copies:
        copy.wait()


HBM, VMEM, FREE = "hbm", "vmem", "free"


def call(kernel, in_specs, outs, scratch, name, flops, args):
    moved = sum(a.size * a.dtype.itemsize for a in args)
    moved += sum(s.size * s.dtype.itemsize for s, _ in outs)
    spaces = {HBM: pltpu.HBM, VMEM: pltpu.VMEM}
    where = {key: pl.BlockSpec(memory_space=spaces.get(key, pltpu.VMEM)) for key in (HBM, VMEM, FREE)}
    args = [
        pltpu.with_memory_space_constraint(a, spaces[spec]) if spec in spaces else a
        for a, spec in zip(args, in_specs)
    ]
    return pl.pallas_call(
        kernel,
        in_specs=[where[spec] for spec in in_specs],
        out_specs=[where[spec] for _, spec in outs],
        out_shape=[
            pltpu.VMEM(shape.shape, shape.dtype) if spec is VMEM else shape for shape, spec in outs
        ],
        scratch_shapes=scratch,
        compiler_params=pltpu.CompilerParams(vmem_limit_bytes=20 << 20),
        cost_estimate=pl.CostEstimate(flops=flops, bytes_accessed=moved, transcendentals=0),
        name=name,
    )(*args)


def swap(value, distance):
    count = lax.axis_size("seq")
    route = [(i, i ^ distance) for i in range(count) if i ^ distance < count]
    return lax.ppermute(value, "seq", route)


def chip_kernel(positions, total, partner, rates_pc, chip, message, rates):
    half = chip.shape[1]
    upper = lax.axis_index("seq") % 2
    at = pl.ds(pl.multiple_of(upper * half, LANES), half)
    mine, theirs = total[:, at], partner[:, at].astype(F32)
    rate = rates_pc[:, at]
    above = upper == 1
    whole = jnp.exp(-rate * positions) * jnp.where(above, theirs, mine)
    whole += jnp.where(above, mine, theirs)
    chip[...] = whole
    message[...] = whole.astype(BF16)
    rates[...] = rate


def round_kernel(positions, size, last, chip, received, before, rates, chip_out, before_out, message):
    index = lax.axis_index("seq")
    above = (index // size) % 2 == 1
    behind = ((index % size) // 2 * 2 * positions).astype(F32)
    theirs = received[...].astype(F32)
    rate = rates[...]
    mine = chip[...]
    earlier = before[...] + jnp.where(above, jnp.exp(-rate * behind) * theirs, 0.0)
    before_out[...] = earlier
    whole = jnp.exp(-rate * (positions * size)) * jnp.where(above, theirs, mine)
    whole += jnp.where(above, mine, theirs)
    chip_out[...] = whole
    message[...] = (earlier if last else whole).astype(BF16)


def scan_states(total, message, rates_pc, positions, fill):
    count = lax.axis_size("seq")
    poles, features = total.shape
    half = jax.ShapeDtypeStruct((poles, features // 2), F32)
    packed = jax.ShapeDtypeStruct((poles, features // 2), BF16)
    partner = swap(fill(message), 1)
    chip, message, rates = call(
        functools.partial(chip_kernel, positions), [VMEM] * 3,
        [(half, VMEM), (packed, VMEM), (half, VMEM)], [], "chip", total.size, (total, partner, rates_pc),
    )
    before = jnp.zeros_like(chip)
    if count == 2:
        message = jnp.zeros_like(message)
    size = 2
    while size < count:
        received = swap(fill(message), size)
        chip, before, message = call(
            functools.partial(round_kernel, positions, size, 2 * size >= count),
            [VMEM, VMEM, FREE if size == 2 else VMEM, VMEM],
            [(half, VMEM), (half, VMEM), (packed, VMEM)],
            [], "round", total.size, (chip, received, before, rates),
        )
        size *= 2
    return before, swap(fill(message), 1), partner


def shards(
    gate_out, gate_in, values, gate_mid, medium_taps, medium_skip, residues, rates, long_skip
):
    row_count, features = gate_out.shape
    groups, poles = rates.shape
    per_group = features // groups
    count = lax.axis_size("seq")
    width = features // PIECES
    shape = jax.ShapeDtypeStruct
    dma = pltpu.SemaphoreType.DMA
    chunks = features // CHUNK

    tail = (gate_in[row_count - SUB :].astype(F32) * values[row_count - SUB :].astype(F32)).astype(
        BF16
    )
    halo = lax.ppermute(tail, "seq", [(i, i + 1) for i in range(count - 1)])

    rate_rows = rates.reshape(-1, LANES)
    residue_rows = residues.reshape(-1, LANES)
    med_skip = medium_skip[None]
    lng_skip = long_skip[None]
    per_pole = shape((poles, features), F32)
    half_rows = shape((SUB, features), BF16)

    med_strips, folds, rates_pc, product, mid_first, gated_b, later = call(
        functools.partial(early_kernel, per_group, poles),
        [HBM, HBM, HBM, FREE, FREE, FREE],
        [
            (shape((groups * STRIP, MED + STRIP), BF16), VMEM),
            (shape((groups * poles, SUB), BF16), VMEM),
            (per_pole, VMEM),
            (half_rows, VMEM),
            (half_rows, VMEM),
            (half_rows, VMEM),
            (per_pole, VMEM),
        ],
        [
            pltpu.VMEM((row_count, features), BF16),
            pltpu.VMEM((row_count, features), BF16),
            pltpu.VMEM((SUB, features), BF16),
            pltpu.VMEM((groups, 2 * LANES), F32),
            pltpu.VMEM((2 * SUB, WIDE), BF16),
            dma((chunks, 4)),
        ],
        "early",
        2 * SUB * SUB * features * 8,
        (gate_in, values, gate_mid, medium_taps, rate_rows, med_skip),
    )
    gated_a, first, total, message = call(
        functools.partial(late_kernel, per_group, poles),
        [VMEM] * 6 + [FREE, VMEM],
        [(half_rows, VMEM), (per_pole, VMEM), (per_pole, VMEM), (shape((poles, features), BF16), VMEM)],
        [pltpu.VMEM((2 * SUB, WIDE), BF16)],
        "late",
        2 * SUB * SUB * features * 8,
        (halo, product, mid_first, med_strips, folds, rates_pc, med_skip, later),
    )

    def inner(piece, rate_rows):
        return call(
            functools.partial(inner_kernel, per_group, poles, piece * width),
            [VMEM, VMEM, FREE, FREE, FREE, HBM],
            [
                (shape((row_count, width), F32), VMEM),
                (shape((SUB, width), BF16), VMEM),
                (shape((row_count, width), BF16), VMEM),
                (shape((1, LANES), F32), VMEM),
            ],
            [
                pltpu.VMEM((width // per_group, LANES), BF16),
                pltpu.VMEM((width // per_group, 2 * LANES), F32),
                pltpu.VMEM((2, 2 * SUB - STRIP, WIDE), BF16),
                dma,
            ],
            f"inner{piece}",
            4 * SUB * SUB * width * 8,
            (gated_a, gated_b, rate_rows, residue_rows, lng_skip, gate_out),
        )

    pieces = []

    def fill(message):
        if len(pieces) < PIECES:
            tokens = [piece[-1] for piece in pieces]
            message, held, _ = lax.optimization_barrier((message, rate_rows, tokens))
            pieces.append(inner(len(pieces), held))
        else:
            message, _ = lax.optimization_barrier((message, pieces[-1][-1]))
        return message

    before, other, partner = scan_states(total, message, rates_pc, row_count, fill)
    while len(pieces) < PIECES:
        fill(message)
    parts, lifts, gates, _ = zip(*pieces)
    (mixed,) = call(
        functools.partial(final_kernel, per_group, poles),
        [VMEM] * (5 + 3 * PIECES),
        [(shape((row_count, features), BF16), HBM)],
        [pltpu.VMEM((row_count, features), BF16), dma((PIECES,))],
        "final",
        2 * SUB * SUB * features * 2,
        (before, other, partner, first, rates_pc, *parts, *lifts, *gates),
    )
    return mixed


def solution(mesh):
    rows = P(("grp", "seq"), None)
    return jax.shard_map(
        shards,
        mesh=mesh,
        in_specs=(rows,) * 4 + (P(),) * 5,
        out_specs=rows,
        check_vma=False,
    )
```

time: 87.1 us -> 56.5 us (0.65)
  Pallas kernels: 49.1 us -> 31 us
  local copies, waits for them, and re-layouts: 9.54 us -> 1.86 us
  waiting for transfers between devices: 9.23 us -> 4.95 us
  other arithmetic: 4.22 us -> 2.79 us
  starting transfers between devices: 13.8 us -> 15 us
    pallas_call x4 -> x11, Pallas kernels: 49.1 us -> 31 us  [call(): pl.pallas_call(kernel, in_specs=[where[spec] for spec in in_specs], out_s...]
    unnamed x42 -> x20, local copies, waits for them, and re-layouts: 9.34 us -> 1.65 us
    ppermute x5, waiting for transfers between devices: 9.22 us -> 4.94 us  [swap(): return lax.ppermute(value, 'seq', route)]
    ppermute x5, starting transfers between devices: 9.64 us -> 12.6 us  [swap(): return lax.ppermute(value, 'seq', route)]
    ppermute x2 -> x1, starting transfers between devices: 4.13 us -> 2.46 us  [shards(): halo = lax.ppermute(tail, 'seq', [(i, i + 1) for i in range(count - 1)])]
    convert_element_type x5 -> x0, other arithmetic: 1.18 us -> none  [the longest x3 1.06 us: scan_states(): theirs = swap(chip.astype(BF16), size).astype(F32)]
  transfers between devices with their start and end apart: 7 -> 6, of which waited for: 4 -> 3; matrix products, arithmetic and copies ran while one was open for 1% -> 1% of each run, Pallas kernels for 33% -> 35%
where the time goes in v2:
time: 56.5 us; the launch traced here: 56 us
  Pallas kernels  31 us (55%)
  starting transfers between devices  15 us (27%)
  waiting for transfers between devices  4.95 us (9%)
  other arithmetic  2.79 us (5%)
  local copies, waits for them, and re-layouts  1.86 us (3%)
    pallas_call x11, Pallas kernels, call(): pl.pallas_call(kernel, in_specs=[where[spec] for spec in in_specs], out_s...  31 us
    ppermute x5, starting transfers between devices, swap(): return lax.ppermute(value, 'seq', route)  12.6 us
    ppermute x5, waiting for transfers between devices, swap(): return lax.ppermute(value, 'seq', route)  4.94 us
    convert_element_type x1, other arithmetic, shards(): (gate_in[row_count - SUB:].astype(F32) * values[row_count - SUB:].astype(...  2.79 us
    ppermute x1, starting transfers between devices, shards(): halo = lax.ppermute(tail, 'seq', [(i, i + 1) for i in range(count - 1)])  2.46 us
    unnamed x20, local copies, waits for them, and re-layouts  1.65 us
  transfers between devices with their start and end apart: 6, of which 3 were waited for; matrix products, arithmetic and copies ran while one was open for 1% of the time, Pallas kernels for 35%

profile of v2, /device:TPU:0, one launch (start us, length us, event | category | flops | bytes accessed | tf_op | source)
XLA Modules:
  0.0 56.0 jit_solution(16766125617622246857)
XLA Ops:
  0.0 2.8 %multiply_convert_fusion = bf16[128,4096]{1,0:T(8,128)(2,1)} fusion(bf16[256,4096]{1,0:T(8,128)(2,1)} %values.1, bf16[256,4096]{1,0:T(8,128)(2,1)} %gate_in.1), kind=kLoop, calls=%fused_computation | loop fusion | flops 2097152 | bytes 3145728 | tf_op jit(solution)/shard_map/convert_element_type | solution.py:365
  2.8 2.5 %collective-permute-start = (bf16[128,4096]{1,0:T(8,128)(2,1)}, bf16[128,4096]{1,0:T(8,128)(2,1)S(1)}, u32[]{:S(2)}, u32[]{:S(2)}) collective-permute-start(bf16[128,4096]{1,0:T(8,128)(2,1)} %multiply_convert_fusion), channel_id=1, source_target_pairs={{0,1},{1,2},{2,3},{3,4},{4,5},{5,6},{6,7},{7,8},{8,9},{9,10},{10,1... | collective-permute-start | bytes 3145736 | tf_op jit(solution)/shard_map/ppermute | solution.py:368
  5.3 0.1 copy.12
  5.4 0.1 reshape.6.rates
  5.5 9.8 %early.1 = (bf16[8192,160]{1,0:T(8,128)(2,1)S(1)}, bf16[4096,128]{1,0:T(8,128)(2,1)S(1)}, f32[16,4096]{1,0:T(8,128)S(1)}, bf16[128,4096]{1,0:T(8,128)(2,1)S(1)},...) custom-call(bf16[256,4096]{1,0:T(8,128)(2,1)} %gate_in.1, ...), custom_call_target="tpu_custom_call" | custom-call | flops 1073741824 | bytes 13729792 | tf_op jit(solution)/shard_map/early/pallas_call | solution.py:278
  15.3 0.0 collective-permute-done.halo
  15.3 0.0 copy-start.8
  15.3 0.0 copy-start
  15.3 8.7 %late.1 = (bf16[128,4096]{1,0:T(8,128)(2,1)S(1)}, f32[16,4096]{1,0:T(8,128)S(1)}, f32[16,4096]{1,0:T(8,128)S(1)}, bf16[16,4096]{1,0:T(8,128)(2,1)}) custom-call(bf16[128,4096]{1,0:T(8,128)(2,1)S(1)} %collective-permute-done.halo, bf16[128,4096]{1,0:T(8,128)(2,1)S(1)} %get-tuple-element.49.product, bf16[128,4096]{1,0:T(8,128)(2,1)S(1)} %get-tuple-element.50.gate_mid, ...), custom_call_target="tpu_custom_call" | custom-call | flops 1073741824 | bytes 9060352 | tf_op jit(solution)/shard_map/late/pallas_call | solution.py:278
  24.0 0.7 %copy-done.1 = f32[16,4096]{1,0:T(8,128)} copy-done((f32[16,4096]{1,0:T(8,128)}, f32[16,4096]{1,0:T(8,128)S(1)}, u32[]{:S(2)}) %copy-start.1) | copy-done | bytes 262168
  24.7 0.7 %copy-done.3 = f32[16,4096]{1,0:T(8,128)} copy-done((f32[16,4096]{1,0:T(8,128)}, f32[16,4096]{1,0:T(8,128)S(1)}, u32[]{:S(2)}) %copy-start.3) | copy-done | bytes 262168
  25.4 4.3 %collective-permute-start.1 = (bf16[16,4096]{1,0:T(8,128)(2,1)}, bf16[16,4096]{1,0:T(8,128)(2,1)S(1)}, u32[]{:S(2)}, u32[]{:S(2)}) collective-permute-start(bf16[16,4096]{1,0:T(8,128)(2,1)} %get-tuple-element.57), channel_id=1, source_target_pairs={{0,1},{1,0},{2,3},{3,2},{4,5},{5,4},{6,7},{7,6},{8,9},{9,8},{10,11... | collective-permute-start | bytes 393224 | tf_op jit(solution)/shard_map/ppermute | solution.py:295
  29.7 0.1 copy.13
  29.8 0.1 reshape.7.residues
  29.9 0.0 copy-start.4
  29.9 3.0 %inner0.1 = (f32[256,1024]{1,0:T(8,128)S(1)}, bf16[128,1024]{1,0:T(8,128)(2,1)S(1)}, bf16[256,1024]{1,0:T(8,128)(2,1)S(1)}, f32[1,128]{1,0:T(1,128)}) custom-call(bf16[128,4096]{1,0:T(8,128)(2,1)S(1)} %get-tuple-element.60.gated_a, bf16[128,4096]{1,0:T(8,128)(2,1)S(1)} %get-tuple-element.61.gated_b, f32[32,128]{1,0:T(8,128)S(1)} %reshape.6.rates, ...), custom_call_target="tpu_custom_call" | custom-call | flops 536870912 | bytes 6078976 | tf_op jit(solution)/shard_map/inner0/pallas_call | solution.py:278
  33.0 0.0 collective-permute-done.1.partner
  33.0 0.1 chip.1
  33.1 2.4 %collective-permute-start.2 = (bf16[16,2048]{1,0:T(8,128)(2,1)S(1)}, bf16[16,2048]{1,0:T(8,128)(2,1)S(1)}, u32[]{:S(2)}, u32[]{:S(2)}) collective-permute-start(bf16[16,2048]{1,0:T(8,128)(2,1)S(1)} %get-tuple-element.64), channel_id=1, source_target_pairs={{0,2},{1,3},{2,0},{3,1},{4,6},{5,7},{6,4},{7,5},{8,10},{9,11},{10,... | collective-permute-start | bytes 196616 | tf_op jit(solution)/shard_map/ppermute | solution.py:295
  35.4 2.3 %inner1.1 = (f32[256,1024]{1,0:T(8,128)S(1)}, bf16[128,1024]{1,0:T(8,128)(2,1)S(1)}, bf16[256,1024]{1,0:T(8,128)(2,1)S(1)}, f32[1,128]{1,0:T(1,128)}) custom-call(bf16[128,4096]{1,0:T(8,128)(2,1)S(1)} %get-tuple-element.60.gated_a, bf16[128,4096]{1,0:T(8,128)(2,1)S(1)} %get-tuple-element.61.gated_b, f32[32,128]{1,0:T(8,128)S(1)} %reshape.6.rates, ...), custom_call_target="tpu_custom_call" | custom-call | flops 536870912 | bytes 6078976 | tf_op jit(solution)/shard_map/inner1/pallas_call | solution.py:278
  37.7 0.4 collective-permute-done.2.received
  38.2 0.1 round.3
  38.3 2.8 %collective-permute-start.3 = (bf16[16,2048]{1,0:T(8,128)(2,1)S(1)}, bf16[16,2048]{1,0:T(8,128)(2,1)S(1)}, u32[]{:S(2)}, u32[]{:S(2)}) collective-permute-start(bf16[16,2048]{1,0:T(8,128)(2,1)S(1)} %get-tuple-element.70), channel_id=1, source_target_pairs={{0,4},{1,5},{2,6},{3,7},{4,0},{5,1},{6,2},{7,3},{8,12},{9,13},{10,... | collective-permute-start | bytes 196616 | tf_op jit(solution)/shard_map/ppermute | solution.py:295
  41.1 2.2 %collective-permute-done.3.received = bf16[16,2048]{1,0:T(8,128)(2,1)S(1)} collective-permute-done((bf16[16,2048]{1,0:T(8,128)(2,1)S(1)}, bf16[16,2048]{1,0:T(8,128)(2,1)S(1)}, u32[]{:S(2)}, u32[]{:S(2)}) %collective-permute-start.3) | collective-permute-done | bytes 65568 | tf_op jit(solution)/shard_map/ppermute | solution.py:295
  43.3 0.1 round.4
  43.4 3.1 %collective-permute-start.4 = (bf16[16,2048]{1,0:T(8,128)(2,1)S(1)}, bf16[16,2048]{1,0:T(8,128)(2,1)S(1)}, u32[]{:S(2)}, u32[]{:S(2)}) collective-permute-start(bf16[16,2048]{1,0:T(8,128)(2,1)S(1)} %get-tuple-element.74), channel_id=1, source_target_pairs={{0,8},{1,9},{2,10},{3,11},{4,12},{5,13},{6,14},{7,15},{8,0},{9,1},... | collective-permute-start | bytes 196616 | tf_op jit(solution)/shard_map/ppermute | solution.py:295
  46.5 2.2 %collective-permute-done.4.received = bf16[16,2048]{1,0:T(8,128)(2,1)S(1)} collective-permute-done((bf16[16,2048]{1,0:T(8,128)(2,1)S(1)}, bf16[16,2048]{1,0:T(8,128)(2,1)S(1)}, u32[]{:S(2)}, u32[]{:S(2)}) %collective-permute-start.4) | collective-permute-done | bytes 65568 | tf_op jit(solution)/shard_map/ppermute | solution.py:295
  48.8 0.7 %round.5 = (f32[16,2048]{1,0:T(8,128)}, f32[16,2048]{1,0:T(8,128)S(1)}, bf16[16,2048]{1,0:T(8,128)(2,1)S(1)}) custom-call(f32[16,2048]{1,0:T(8,128)S(1)} %get-tuple-element.72.chip, bf16[16,2048]{1,0:T(8,128)(2,1)S(1)} %collective-permute-done.4.received, f32[16,2048]{1,0:T(8,128)S(1)} %get-tuple-element.75.before, f32[16,2048]{1,0:T(8,128)S(1)} %get-tuple-element.65.rates), custom_call_target="tpu_custom_call" | custom-call | flops 65536 | bytes 786432 | tf_op jit(solution)/shard_map/round/pallas_call | solution.py:278
  49.5 0.0 collective-permute-start.5
  49.5 2.3 %inner2.1 = (f32[256,1024]{1,0:T(8,128)S(1)}, bf16[128,1024]{1,0:T(8,128)(2,1)S(1)}, bf16[256,1024]{1,0:T(8,128)(2,1)S(1)}, f32[1,128]{1,0:T(1,128)}) custom-call(bf16[128,4096]{1,0:T(8,128)(2,1)S(1)} %get-tuple-element.60.gated_a, bf16[128,4096]{1,0:T(8,128)(2,1)S(1)} %get-tuple-element.61.gated_b, f32[32,128]{1,0:T(8,128)S(1)} %reshape.6.rates, ...), custom_call_target="tpu_custom_call" | custom-call | flops 536870912 | bytes 6078976 | tf_op jit(solution)/shard_map/inner2/pallas_call | solution.py:278
  51.8 2.3 %inner3.1 = (f32[256,1024]{1,0:T(8,128)S(1)}, bf16[128,1024]{1,0:T(8,128)(2,1)S(1)}, bf16[256,1024]{1,0:T(8,128)(2,1)S(1)}, f32[1,128]{1,0:T(1,128)}) custom-call(bf16[128,4096]{1,0:T(8,128)(2,1)S(1)} %get-tuple-element.60.gated_a, bf16[128,4096]{1,0:T(8,128)(2,1)S(1)} %get-tuple-element.61.gated_b, f32[32,128]{1,0:T(8,128)S(1)} %reshape.6.rates, ...), custom_call_target="tpu_custom_call" | custom-call | flops 536870912 | bytes 6078976 | tf_op jit(solution)/shard_map/inner3/pallas_call | solution.py:278
  54.1 1.8 %final.1 = bf16[256,4096]{1,0:T(8,128)(2,1)} custom-call(f32[16,2048]{1,0:T(8,128)S(1)} %get-tuple-element.76.own, bf16[16,2048]{1,0:T(8,128)(2,1)S(1)} %collective-permute-done.5.other, bf16[16,4096]{1,0:T(8,128)(2,1)S(1)} %collective-permute-done.1.partner, f32[16,4096]{1,0:T(8,128)S(1)} %copy-done.2, f32[16,4096]{1,0:T(8,128)S(1)} %get-tuple-element.53.rates_pc, ...), custom_call_target="tpu_custom_call" | custom-call | flops 268435456 | bytes 10289152 | tf_op jit(solution)/shard_map/final/pallas_call | solution.py:278
  (15 shorter events, 0.0 us)
Async XLA Ops:
  0.0 5.3 %copy-start.7 = (f32[256,16]{0,1:T(8,128)S(1)}, f32[256,16]{0,1:T(8,128)}, u32[]{:S(2)}) copy-start(f32[256,16]{0,1:T(8,128)} %param.16) | copy-start | bytes 49156
  0.0 5.5 %copy-start.6 = (f32[4096]{0:T(1024)S(1)}, f32[4096]{0:T(1024)}, u32[]{:S(2)}) copy-start(f32[4096]{0:T(1024)} %param.14) | copy-start | bytes 49156
  0.0 5.5 %copy-start.5 = (bf16[256,128]{1,0:T(8,128)(2,1)S(1)}, bf16[256,128]{1,0:T(8,128)(2,1)}, u32[]{:S(2)}) copy-start(bf16[256,128]{1,0:T(8,128)(2,1)} %taps.1) | copy-start | bytes 196612
  2.8 12.5 %collective-permute-start = (bf16[128,4096]{1,0:T(8,128)(2,1)}, bf16[128,4096]{1,0:T(8,128)(2,1)S(1)}, u32[]{:S(2)}, u32[]{:S(2)}) collective-permute-start(bf16[128,4096]{1,0:T(8,128)(2,1)} %multiply_convert_fusion), channel_id=1, source_target_pairs={{0,1},{1,2},{2,3},{3,4},{4,5},{5,6},{6,7},{7,8},{8,9},{9,10},{10,1... | collective-permute-start | bytes 3145736 | tf_op jit(solution)/shard_map/ppermute | solution.py:368
  15.3 14.4 %copy-start.8 = (f32[256,16]{0,1:T(8,128)S(1)}, f32[256,16]{0,1:T(8,128)}, u32[]{:S(2)}) copy-start(f32[256,16]{0,1:T(8,128)} %param.15) | copy-start | bytes 49156
  15.3 14.6 %copy-start = (f32[4096]{0:T(1024)S(1)}, f32[4096]{0:T(1024)}, u32[]{:S(2)}) copy-start(f32[4096]{0:T(1024)} %param.17) | copy-start | bytes 49156
  24.0 0.7 %copy-start.1 = (f32[16,4096]{1,0:T(8,128)}, f32[16,4096]{1,0:T(8,128)S(1)}, u32[]{:S(2)}) copy-start(f32[16,4096]{1,0:T(8,128)S(1)} %get-tuple-element.78.state) | copy-start | bytes 786436
  24.7 0.7 %copy-start.3 = (f32[16,4096]{1,0:T(8,128)}, f32[16,4096]{1,0:T(8,128)S(1)}, u32[]{:S(2)}) copy-start(f32[16,4096]{1,0:T(8,128)S(1)} %get-tuple-element.55.total) | copy-start | bytes 786436
  25.4 7.6 %collective-permute-start.1 = (bf16[16,4096]{1,0:T(8,128)(2,1)}, bf16[16,4096]{1,0:T(8,128)(2,1)S(1)}, u32[]{:S(2)}, u32[]{:S(2)}) collective-permute-start(bf16[16,4096]{1,0:T(8,128)(2,1)} %get-tuple-element.57), channel_id=1, source_target_pairs={{0,1},{1,0},{2,3},{3,2},{4,5},{5,4},{6,7},{7,6},{8,9},{9,8},{10,11... | collective-permute-start | bytes 393224 | tf_op jit(solution)/shard_map/ppermute | solution.py:295
  29.9 3.1 %copy-start.4 = (f32[16,4096]{1,0:T(8,128)S(1)}, f32[16,4096]{1,0:T(8,128)}, u32[]{:S(2)}) copy-start(f32[16,4096]{1,0:T(8,128)} %copy-done.3) | copy-start | bytes 786436
  33.1 5.1 %collective-permute-start.2 = (bf16[16,2048]{1,0:T(8,128)(2,1)S(1)}, bf16[16,2048]{1,0:T(8,128)(2,1)S(1)}, u32[]{:S(2)}, u32[]{:S(2)}) collective-permute-start(bf16[16,2048]{1,0:T(8,128)(2,1)S(1)} %get-tuple-element.64), channel_id=1, source_target_pairs={{0,2},{1,3},{2,0},{3,1},{4,6},{5,7},{6,4},{7,5},{8,10},{9,11},{10,... | collective-permute-start | bytes 196616 | tf_op jit(solution)/shard_map/ppermute | solution.py:295
  38.3 5.0 %collective-permute-start.3 = (bf16[16,2048]{1,0:T(8,128)(2,1)S(1)}, bf16[16,2048]{1,0:T(8,128)(2,1)S(1)}, u32[]{:S(2)}, u32[]{:S(2)}) collective-permute-start(bf16[16,2048]{1,0:T(8,128)(2,1)S(1)} %get-tuple-element.70), channel_id=1, source_target_pairs={{0,4},{1,5},{2,6},{3,7},{4,0},{5,1},{6,2},{7,3},{8,12},{9,13},{10,... | collective-permute-start | bytes 196616 | tf_op jit(solution)/shard_map/ppermute | solution.py:295
  43.4 5.3 %collective-permute-start.4 = (bf16[16,2048]{1,0:T(8,128)(2,1)S(1)}, bf16[16,2048]{1,0:T(8,128)(2,1)S(1)}, u32[]{:S(2)}, u32[]{:S(2)}) collective-permute-start(bf16[16,2048]{1,0:T(8,128)(2,1)S(1)} %get-tuple-element.74), channel_id=1, source_target_pairs={{0,8},{1,9},{2,10},{3,11},{4,12},{5,13},{6,14},{7,15},{8,0},{9,1},... | collective-permute-start | bytes 196616 | tf_op jit(solution)/shard_map/ppermute | solution.py:295
  49.5 4.6 %collective-permute-start.5 = (bf16[16,2048]{1,0:T(8,128)(2,1)S(1)}, bf16[16,2048]{1,0:T(8,128)(2,1)S(1)}, u32[]{:S(2)}, u32[]{:S(2)}) collective-permute-start(bf16[16,2048]{1,0:T(8,128)(2,1)S(1)} %get-tuple-element.77), channel_id=1, source_target_pairs={{0,1},{1,0},{2,3},{3,2},{4,5},{5,4},{6,7},{7,6},{8,9},{9,8},{10,11... | collective-permute-start | bytes 196616 | tf_op jit(solution)/shard_map/ppermute | solution.py:295
  51.8 2.3 %copy-start.2 = (f32[16,4096]{1,0:T(8,128)S(1)}, f32[16,4096]{1,0:T(8,128)}, u32[]{:S(2)}) copy-start(f32[16,4096]{1,0:T(8,128)} %copy-done.1) | copy-start | bytes 786436

commit v3 on v2

v3 whole, which is shorter than its diff:
```python
import functools

import jax
import jax.numpy as jnp
from jax import lax
from jax.experimental import pallas as pl
from jax.experimental.pallas import tpu as pltpu
from jax.sharding import PartitionSpec as P

MED = 128
SUB = 128
STRIP = 32
LANES = 128
WIDE = 1024
CHUNK = 1024
PIECES = 3
BF16 = jnp.bfloat16
F32 = jnp.float32


def dot(a, b, precision=None):
    return jnp.dot(a, b, preferred_element_type=F32, precision=precision)


def own_groups(stack, rows, per_group):
    groups = stack.shape[0] // rows
    owner = lax.broadcasted_iota(jnp.int32, (rows, stack.shape[1]), 1) % LANES // per_group
    kept = stack[:rows]
    for g in range(1, groups):
        kept = jnp.where(owner == g, stack[g * rows : (g + 1) * rows], kept)
    return kept


def toeplitz(line, g):
    spread = jnp.broadcast_to(line[g : g + 1], (STRIP, 2 * LANES))
    return pltpu.roll(spread, 0, 1, stride=1, stride_axis=0)


def filter_block(strips, window, depth, per_group):
    rows = []
    for i in range(0, SUB // STRIP, 2):
        first, second = i * STRIP, (i + 1) * STRIP
        spans = jnp.concatenate([window[first : first + depth], window[second : second + depth]], axis=1)
        both = own_groups(dot(strips, spans), STRIP, per_group)
        rows += [both[:, :LANES], both[:, LANES:]]
    return jnp.concatenate(rows, axis=0)


def lanes_at(step, b):
    return pl.ds(pl.multiple_of(step * WIDE + b * LANES, LANES), LANES)


def rows_at(step, b, rows_per_block):
    start = (step * (WIDE // LANES) + b) * rows_per_block
    return pl.ds(pl.multiple_of(start, rows_per_block), rows_per_block)


def tail_kernel(gate_in, values, product, held, sems):
    last, features = gate_in.shape[0] - SUB, gate_in.shape[1]
    copies = []
    for c in range(features // CHUNK):
        lanes = pl.ds(c * CHUNK, CHUNK)
        for k, source in enumerate((gate_in, values)):
            copy = pltpu.make_async_copy(
                source.at[pl.ds(last, SUB), lanes], held.at[k, :, lanes], sems.at[c, k]
            )
            copy.start()
            copies.append(copy)
    for c in range(features // CHUNK):
        copies[2 * c].wait()
        copies[2 * c + 1].wait()
        lanes = slice(c * CHUNK, (c + 1) * CHUNK)
        product[:, lanes] = (held[0, :, lanes].astype(F32) * held[1, :, lanes].astype(F32)).astype(
            BF16
        )


def early_kernel(
    per_group, poles,
    gate_in, values, gate_mid, taps, rates, med_skip,
    med_strips, folds, rates_pc, product, mid_first, gated_out, state,
    in_buf, value_buf, mid_buf, line, sems,
):
    features = gate_in.shape[1]
    block = LANES // per_group
    copies = []
    for c in range(features // CHUNK):
        lanes = pl.ds(c * CHUNK, CHUNK)
        copies.append(
            [
                pltpu.make_async_copy(gate_in.at[:, lanes], in_buf.at[:, lanes], sems.at[c, 0]),
                pltpu.make_async_copy(values.at[:, lanes], value_buf.at[:, lanes], sems.at[c, 1]),
                pltpu.make_async_copy(
                    gate_mid.at[pl.ds(SUB, SUB), lanes], mid_buf.at[:, lanes], sems.at[c, 2]
                ),
                pltpu.make_async_copy(
                    gate_mid.at[pl.ds(0, SUB), lanes], mid_first.at[:, lanes], sems.at[c, 3]
                ),
            ]
        )
        for copy in copies[-1]:
            copy.start()
    tap = lax.broadcasted_iota(jnp.int32, (LANES, 2 * LANES), 0)
    spot = lax.broadcasted_iota(jnp.int32, (LANES, 2 * LANES), 1)
    line[...] = dot(taps[...], (spot == MED - tap).astype(BF16))
    offset = lax.broadcasted_iota(jnp.int32, (LANES, LANES), 1).astype(F32)

    def one(step):
        for b in range(WIDE // LANES):
            at = lanes_at(step, b)
            rate_row = rates[pl.ds(step * (WIDE // LANES) + b, 1), :]
            rate_col = jnp.transpose(jnp.broadcast_to(rate_row, (LANES, LANES)))
            rates_pc[:, at] = own_groups(rate_col, poles, per_group)
            fold = jnp.exp(-rate_col * (SUB - 1.0 - offset)).astype(BF16)
            folds[rows_at(step, b, LANES), :] = fold
            first = (step * (WIDE // LANES) + b) * block
            lines = line[pl.ds(pl.multiple_of(first, block), block), :]
            strips = jnp.concatenate(
                [toeplitz(lines, g)[:, : MED + STRIP].astype(BF16) for g in range(block)], axis=0
            )
            med_strips[rows_at(step, b, block * STRIP), :] = strips
            rows = (in_buf[:, at].astype(F32) * value_buf[:, at].astype(F32)).astype(BF16)
            product[:, at] = rows[:SUB]
            medium = filter_block(strips, rows, MED + STRIP, per_group)
            medium = medium + med_skip[:, at] * rows[SUB:].astype(F32)
            gated = (mid_buf[:, at].astype(F32) * medium).astype(BF16)
            gated_out[:, at] = gated
            state[:, at] = own_groups(dot(fold, gated), poles, per_group)

    for c in range(features // CHUNK):
        for copy in copies[c]:
            copy.wait()
        pl.loop(c * (CHUNK // WIDE), (c + 1) * (CHUNK // WIDE))(one)


def late_kernel(
    per_group, poles, followed,
    halo, product, gate_mid, med_strips, folds, rates_pc, med_skip, later,
    gated_out, state, total, message,
):
    half = total.shape[1]
    block = LANES // per_group
    side = lax.axis_index("seq") % 2
    side = side if followed else 1 - side

    base = pl.multiple_of(side * half, half)
    for b in range(half // LANES):
        at = pl.ds(pl.multiple_of(base + b * LANES, LANES), LANES)
        to = slice(b * LANES, (b + 1) * LANES)
        tall = block * STRIP
        spot = pl.multiple_of(side * (half // LANES * tall), tall) + b * tall
        rows = product[:, at]
        window = jnp.concatenate([halo[:, at], rows], axis=0)
        strips = med_strips[pl.ds(pl.multiple_of(spot, tall), tall), :]
        medium = filter_block(strips, window, MED + STRIP, per_group)
        medium = medium + med_skip[:, at] * rows.astype(F32)
        gated = (gate_mid[:, at].astype(F32) * medium).astype(BF16)
        gated_out[:, to] = gated
        first = own_groups(dot(folds[at, :], gated), poles, per_group)
        state[:, to] = first
        whole = jnp.exp(-rates_pc[:, at] * SUB) * first + later[:, at]
        total[:, to] = whole
        message[:, to] = whole.astype(BF16)


def column(row):
    return jnp.transpose(jnp.broadcast_to(row, (LANES, LANES)))


def inner_kernel(
    per_group, poles, base,
    other_a, own_a, gated_b, rates, residues, long_skip, gate_out,
    part, lift, gate_copy, token,
    taps, line, gated_a, sem,
):
    width = part.shape[1]
    half = own_a.shape[1]
    upper = lax.axis_index("seq") % 2
    block = LANES // per_group
    for core in range(2):

        @pl.when(upper == core)
        def _():
            for b in range(width // LANES):
                side, inside = divmod(base + b * LANES, half)
                source = own_a if side == core else other_a
                gated_a[:, b * LANES : (b + 1) * LANES] = source[:, inside : inside + LANES]

    copy = pltpu.make_async_copy(gate_out.at[:, pl.ds(base, width)], gate_copy, sem)
    copy.start()
    offset = lax.broadcasted_iota(jnp.int32, (LANES, LANES), 1).astype(F32)
    after = lax.broadcasted_iota(jnp.int32, (SUB, LANES), 0).astype(F32) + 1.0
    for b in range(width // LANES):
        row = slice(base // LANES + b, base // LANES + b + 1)
        rate_row = rates[row, :]
        residue_row = residues[row, :]
        here = slice(b * LANES, (b + 1) * LANES)
        lift[:, here] = (residue_row * jnp.exp(-rate_row * after)).astype(BF16)
        terms = column(residue_row) * jnp.exp(-column(rate_row) * offset)
        taps[b * block : (b + 1) * block, :] = jnp.sum(
            terms.reshape(block, poles, LANES), axis=1
        ).astype(BF16)
    tap = lax.broadcasted_iota(jnp.int32, (LANES, 2 * LANES), 0)
    spot = lax.broadcasted_iota(jnp.int32, (LANES, 2 * LANES), 1)
    turn = (spot == (SUB - STRIP - tap + 2 * LANES) % (2 * LANES)).astype(BF16)
    line[...] = dot(taps[...], turn)

    for b in range(width // LANES):
        at = slice(b * LANES, (b + 1) * LANES)
        source = slice(base + b * LANES, base + (b + 1) * LANES)
        lines = line[b * block : (b + 1) * block, :]
        strips = jnp.concatenate(
            [toeplitz(lines, g)[:, :LANES].astype(BF16) for g in range(block)], axis=0
        )
        for k, rows in enumerate((gated_a[:, at], gated_b[:, source])):
            window = jnp.concatenate([jnp.zeros((SUB - STRIP, LANES), BF16), rows], axis=0)
            part[k * SUB : (k + 1) * SUB, at] = filter_block(
                strips, window, SUB, per_group
            ) + long_skip[:, source] * rows.astype(F32)

    token[...] = part[:1, :LANES]
    copy.wait()


def spread_groups(state, per_group, poles):
    tall = jnp.concatenate([state] * (LANES // per_group), axis=0)
    owner = lax.broadcasted_iota(jnp.int32, tall.shape, 1) // per_group
    mine = lax.broadcasted_iota(jnp.int32, tall.shape, 0) // poles
    return jnp.where(owner == mine, tall, 0.0).astype(BF16)


def final_kernel(per_group, poles, own, other, own_state, other_state, rates_pc, *refs):
    parts, lifts, gates = (refs[k * PIECES : (k + 1) * PIECES] for k in range(3))
    mixed, out, sems = refs[3 * PIECES :]
    half = own.shape[1]
    upper = lax.axis_index("seq") % 2
    copies = []
    base = 0
    for piece, (part, lift, gate) in enumerate(zip(parts, lifts, gates)):
        width = part.shape[1]
        for b in range(width // LANES):
            at = slice(b * LANES, (b + 1) * LANES)
            to = slice(base + b * LANES, base + (b + 1) * LANES)
            side, inside = divmod(base + b * LANES, half)
            inside = slice(inside, inside + LANES)
            mine = upper == side
            start = jnp.where(mine, own[:, inside], other[:, inside].astype(F32))
            state = jnp.where(mine, own_state[:, inside], other_state[:, inside])
            middle = jnp.exp(-rates_pc[:, to] * SUB) * start + state
            before = jnp.concatenate(
                [spread_groups(start, per_group, poles), spread_groups(middle, per_group, poles)],
                axis=1,
            )
            lifted = dot(lift[:, at], before)
            for k in range(2):
                rows = slice(k * SUB, (k + 1) * SUB)
                long_out = part[rows, at] + lifted[:, k * LANES : (k + 1) * LANES]
                out[rows, to] = (gate[rows, at].astype(F32) * long_out).astype(BF16)
        lanes = pl.ds(base, width)
        copies.append(pltpu.make_async_copy(out.at[:, lanes], mixed.at[:, lanes], sems.at[piece]))
        copies[-1].start()
        base += width
    for copy in copies:
        copy.wait()


HBM, VMEM, FREE = "hbm", "vmem", "free"


def call(kernel, in_specs, outs, scratch, name, flops, args):
    moved = sum(a.size * a.dtype.itemsize for a in args)
    moved += sum(s.size * s.dtype.itemsize for s, _ in outs)
    spaces = {HBM: pltpu.HBM, VMEM: pltpu.VMEM}
    where = {key: pl.BlockSpec(memory_space=spaces.get(key, pltpu.VMEM)) for key in (HBM, VMEM, FREE)}
    args = [
        pltpu.with_memory_space_constraint(a, spaces[spec]) if spec in spaces else a
        for a, spec in zip(args, in_specs)
    ]
    return pl.pallas_call(
        kernel,
        in_specs=[where[spec] for spec in in_specs],
        out_specs=[where[spec] for _, spec in outs],
        out_shape=[
            pltpu.VMEM(shape.shape, shape.dtype) if spec is VMEM else shape for shape, spec in outs
        ],
        scratch_shapes=scratch,
        compiler_params=pltpu.CompilerParams(vmem_limit_bytes=20 << 20),
        cost_estimate=pl.CostEstimate(flops=flops, bytes_accessed=moved, transcendentals=0),
        name=name,
    )(*args)


def swap(value, distance):
    count = lax.axis_size("seq")
    route = [(i, i ^ distance) for i in range(count) if i ^ distance < count]
    return lax.ppermute(value, "seq", route)


def chip_kernel(positions, total, partner, rates_pc, chip, before, message, rates):
    half = chip.shape[1]
    upper = lax.axis_index("seq") % 2
    above = upper == 1
    mine, theirs = total[...], partner[...].astype(F32)
    rate = rates_pc[:, pl.ds(pl.multiple_of(upper * half, LANES), half)]
    whole = jnp.exp(-rate * positions) * jnp.where(above, theirs, mine)
    whole += jnp.where(above, mine, theirs)
    chip[...] = whole
    before[...] = jnp.zeros_like(whole)
    message[...] = whole.astype(BF16)
    rates[...] = rate


def grown(positions, size, chip, received, before, rates):
    index = lax.axis_index("seq")
    above = (index // size) % 2 == 1
    behind = ((index % size) // 2 * 2 * positions).astype(F32)
    rate, mine, theirs = rates[...], chip[...], received[...].astype(F32)
    earlier = before[...] + jnp.where(above, jnp.exp(-rate * behind) * theirs, 0.0)
    whole = jnp.exp(-rate * (positions * size)) * jnp.where(above, theirs, mine)
    return earlier, whole + jnp.where(above, mine, theirs)


def round_kernel(
    positions, size, chip, received, before, rates, _, chip_out, before_out, message
):
    before_out[...], whole = grown(positions, size, chip, received, before, rates)
    chip_out[...] = whole
    message[...] = whole.astype(BF16)


def last_kernel(
    positions, size, chip, received, before, rates, total, partner, _, carry, message
):
    upper = lax.axis_index("seq") % 2 == 1
    earlier, _ = grown(positions, size, chip, received, before, rates)
    lower = jnp.where(upper, partner[...].astype(F32), total[...])
    after = jnp.exp(-rates[...] * positions) * earlier + lower
    carry[...] = jnp.where(upper, after, earlier)
    message[...] = jnp.where(upper, earlier, after).astype(BF16)


def scan_states(total, partner, rates_pc, positions, fill):
    count = lax.axis_size("seq")
    half = jax.ShapeDtypeStruct(total.shape, F32)
    packed = jax.ShapeDtypeStruct(total.shape, BF16)
    chip, before, message, rates = call(
        functools.partial(chip_kernel, positions), [VMEM] * 3,
        [(half, VMEM), (half, VMEM), (packed, VMEM), (half, VMEM)],
        [], "chip", total.size, (total, partner, rates_pc),
    )
    size = 2
    while True:
        message, filled = fill(message)
        received = swap(message, size)
        held = (chip, received, before, rates)
        if 2 * size >= count:
            break
        chip, before, message = call(
            functools.partial(round_kernel, positions, size), [VMEM] * 5,
            [(half, VMEM), (half, VMEM), (packed, VMEM)],
            [], "round", total.size, (*held, filled),
        )
        size *= 2
    carry, message = call(
        functools.partial(last_kernel, positions, size), [VMEM] * 7,
        [(half, VMEM), (packed, VMEM)],
        [], "last", total.size, (*held, total, partner, filled),
    )
    message, _ = fill(message)
    return carry, swap(message, 1)


def shards(
    gate_out, gate_in, values, gate_mid, medium_taps, medium_skip, residues, rates, long_skip
):
    row_count, features = gate_out.shape
    groups, poles = rates.shape
    per_group = features // groups
    count = lax.axis_size("seq")
    cuts = [features // LANES * k // PIECES * LANES for k in range(PIECES + 1)]
    shape = jax.ShapeDtypeStruct
    dma = pltpu.SemaphoreType.DMA
    chunks = features // CHUNK

    (tail,) = call(
        tail_kernel,
        [HBM, HBM],
        [(shape((SUB, features), BF16), VMEM)],
        [pltpu.VMEM((2, SUB, features), BF16), dma((chunks, 2))],
        "tail",
        SUB * features,
        (gate_in, values),
    )
    halo = lax.ppermute(tail, "seq", [(i, i + 1) for i in range(count - 1)])

    rate_rows = rates.reshape(-1, LANES)
    residue_rows = residues.reshape(-1, LANES)
    med_skip = medium_skip[None]
    lng_skip = long_skip[None]
    rate_rows, residue_rows, med_skip, lng_skip = lax.optimization_barrier(
        (rate_rows, residue_rows, med_skip, lng_skip)
    )
    per_pole = shape((poles, features), F32)
    half_rows = shape((SUB, features), BF16)

    med_strips, folds, rates_pc, product, mid_first, gated_b, later = call(
        functools.partial(early_kernel, per_group, poles),
        [HBM, HBM, HBM, FREE, FREE, FREE],
        [
            (shape((groups * STRIP, MED + STRIP), BF16), VMEM),
            (shape((groups * poles, SUB), BF16), VMEM),
            (per_pole, VMEM),
            (half_rows, VMEM),
            (half_rows, VMEM),
            (half_rows, VMEM),
            (per_pole, VMEM),
        ],
        [
            pltpu.VMEM((row_count, features), BF16),
            pltpu.VMEM((row_count, features), BF16),
            pltpu.VMEM((SUB, features), BF16),
            pltpu.VMEM((groups, 2 * LANES), F32),
            dma((chunks, 4)),
        ],
        "early",
        2 * SUB * SUB * features * 8,
        (gate_in, values, gate_mid, medium_taps, rate_rows, med_skip),
    )
    half_states = shape((poles, features // 2), F32)

    def late(followed, med_skip):
        return call(
            functools.partial(late_kernel, per_group, poles, followed),
            [VMEM] * 6 + [FREE, VMEM],
            [
                (shape((SUB, features // 2), BF16), VMEM),
                (half_states, VMEM),
                (half_states, VMEM),
                (shape((poles, features // 2), BF16), VMEM),
            ],
            [],
            "late",
            SUB * SUB * features * 8,
            (halo, product, mid_first, med_strips, folds, rates_pc, med_skip, later),
        )

    other_a, other_state, _, message = late(False, med_skip)
    message, held = lax.optimization_barrier((message, med_skip))
    partner = swap(message, 1)
    own_a, own_state, total, _ = late(True, held)

    def inner(piece, residue_rows):
        width = cuts[piece + 1] - cuts[piece]
        return call(
            functools.partial(inner_kernel, per_group, poles, cuts[piece]),
            [VMEM, VMEM, VMEM, FREE, FREE, FREE, HBM],
            [
                (shape((row_count, width), F32), VMEM),
                (shape((SUB, width), BF16), VMEM),
                (shape((row_count, width), BF16), VMEM),
                (shape((1, LANES), F32), VMEM),
            ],
            [
                pltpu.VMEM((width // per_group, LANES), BF16),
                pltpu.VMEM((width // per_group, 2 * LANES), F32),
                pltpu.VMEM((SUB, width), BF16),
                dma,
            ],
            f"inner{piece}",
            4 * SUB * SUB * width * 8,
            (other_a, own_a, gated_b, rate_rows, residue_rows, lng_skip, gate_out),
        )

    pieces = []

    def fill(message):
        if len(pieces) < PIECES:
            message, held = lax.optimization_barrier((message, residue_rows))
            pieces.append(inner(len(pieces), held))
        return message, pieces[-1][-1]

    carry, other = scan_states(total, partner, rates_pc, row_count, fill)
    while len(pieces) < PIECES:
        fill(other)
    parts, lifts, gates, _ = zip(*pieces)
    (mixed,) = call(
        functools.partial(final_kernel, per_group, poles),
        [VMEM] * (5 + 3 * PIECES),
        [(shape((row_count, features), BF16), HBM)],
        [pltpu.VMEM((row_count, features), BF16), dma((PIECES,))],
        "final",
        2 * SUB * SUB * features * 2,
        (carry, other, own_state, other_state, rates_pc, *parts, *lifts, *gates),
    )
    return mixed


def solution(mesh):
    rows = P(("grp", "seq"), None)
    return jax.shard_map(
        shards,
        mesh=mesh,
        in_specs=(rows,) * 4 + (P(),) * 5,
        out_specs=rows,
        check_vma=False,
    )
```

time: 56.5 us -> 46.4 us (0.82)
  waiting for transfers between devices: 4.95 us -> 1.8 us
  other arithmetic: 2.79 us -> 0 us
  Pallas kernels: 31 us -> 28.3 us
  local copies, waits for them, and re-layouts: 1.86 us -> 0.42 us
    ppermute x5, waiting for transfers between devices: 4.94 us -> 1.8 us  [swap(): return lax.ppermute(value, 'seq', route)]
    convert_element_type x1 -> x0, other arithmetic: 2.79 us -> none  [shards(): (gate_in[row_count - SUB:].astype(F32) * values[row_count - SUB:].astype(...]
    pallas_call x11 -> x12, Pallas kernels: 31 us -> 28.3 us  [call(): pl.pallas_call(kernel, in_specs=[where[spec] for spec in in_specs], out_s...]
    unnamed x20 -> x12, local copies, waits for them, and re-layouts: 1.65 us -> 0.22 us
  transfers between devices with their start and end apart: 6 -> 6, of which waited for: 3 -> 2; matrix products, arithmetic and copies ran while one was open for 1% -> 1% of each run, Pallas kernels for 35% -> 44%
where the time goes in v3:
time: 46.4 us; the launch traced here: 46.2 us
  Pallas kernels  28.3 us (61%)
  starting transfers between devices  15.4 us (33%)
  waiting for transfers between devices  1.8 us (4%)
    pallas_call x12, Pallas kernels, call(): pl.pallas_call(kernel, in_specs=[where[spec] for spec in in_specs], out_s...  28.3 us
    ppermute x5, starting transfers between devices, swap(): return lax.ppermute(value, 'seq', route)  12.9 us
    ppermute x1, starting transfers between devices, shards(): halo = lax.ppermute(tail, 'seq', [(i, i + 1) for i in range(count - 1)])  2.5 us
    ppermute x5, waiting for transfers between devices, swap(): return lax.ppermute(value, 'seq', route)  1.8 us
  transfers between devices with their start and end apart: 6, of which 2 were waited for; matrix products, arithmetic and copies ran while one was open for 1% of the time, Pallas kernels for 44%

profile of v3, /device:TPU:0, one launch (start us, length us, event | category | flops | bytes accessed | tf_op | source)
XLA Modules:
  0.0 46.2 jit_solution(2798917929691330993)
XLA Ops:
  0.0 1.7 %tail.1 = bf16[128,4096]{1,0:T(8,128)(2,1)S(1)} custom-call(bf16[256,4096]{1,0:T(8,128)(2,1)} %gate_in.3, bf16[256,4096]{1,0:T(8,128)(2,1)} %values.3), custom_call_target="tpu_custom_call" | custom-call | flops 524288 | bytes 5242880 | tf_op jit(solution)/shard_map/tail/pallas_call | solution.py:279
  1.7 2.5 %collective-permute-start = (bf16[128,4096]{1,0:T(8,128)(2,1)S(1)}, bf16[128,4096]{1,0:T(8,128)(2,1)S(1)}, u32[]{:S(2)}, u32[]{:S(2)}) collective-permute-start(bf16[128,4096]{1,0:T(8,128)(2,1)S(1)} %tail.1), channel_id=1, source_target_pairs={{0,1},{1,2},{2,3},{3,4},{4,5},{5,6},{6,7},{7,8},{8,9},{9,10},{10,1... | collective-permute-start | bytes 3145736 | tf_op jit(solution)/shard_map/ppermute | solution.py:394
  4.2 0.0 copy-done.3
  4.2 0.1 copy.13
  4.3 0.1 reshape.7.residues
  4.4 0.0 copy-done.4
  4.4 0.1 copy.12
  4.5 0.1 reshape.6.rates
  4.6 0.0 copy-done
  4.6 0.0 copy-done.2
  4.7 9.2 %early.1 = (bf16[8192,160]{1,0:T(8,128)(2,1)S(1)}, bf16[4096,128]{1,0:T(8,128)(2,1)S(1)}, f32[16,4096]{1,0:T(8,128)S(1)}, bf16[128,4096]{1,0:T(8,128)(2,1)S(1)},...) custom-call(bf16[256,4096]{1,0:T(8,128)(2,1)} %gate_in.3, ...), custom_call_target="tpu_custom_call" | custom-call | flops 1073741824 | bytes 13729792 | tf_op jit(solution)/shard_map/early/pallas_call | solution.py:279
  13.8 0.0 collective-permute-done.halo
  13.8 4.3 %late.2 = (bf16[128,2048]{1,0:T(8,128)(2,1)S(1)}, f32[16,2048]{1,0:T(8,128)S(1)}, f32[16,2048]{1,0:T(8,128)}, bf16[16,2048]{1,0:T(8,128)(2,1)S(1)}) custom-call(bf16[128,4096]{1,0:T(8,128)(2,1)S(1)} %collective-permute-done.halo, bf16[128,4096]{1,0:T(8,128)(2,1)S(1)} %get-tuple-element.56.product, bf16[128,4096]{1,0:T(8,128)(2,1)S(1)} %get-tuple-element.57.gate_mid, ...), custom_call_target="tpu_custom_call" | custom-call | flops 536870912 | bytes 8208384 | tf_op jit(solution)/shard_map/late/pallas_call | solution.py:279
  18.1 4.6 %collective-permute-start.1 = (bf16[16,2048]{1,0:T(8,128)(2,1)S(1)}, bf16[16,2048]{1,0:T(8,128)(2,1)S(1)}, u32[]{:S(2)}, u32[]{:S(2)}) collective-permute-start(bf16[16,2048]{1,0:T(8,128)(2,1)S(1)} %get-tuple-element.65), channel_id=1, source_target_pairs={{0,1},{1,0},{2,3},{3,2},{4,5},{5,4},{6,7},{7,6},{8,9},{9,8},{10,11... | collective-permute-start | bytes 196616 | tf_op jit(solution)/shard_map/ppermute | solution.py:296
  22.7 4.2 %late.3 = (bf16[128,2048]{1,0:T(8,128)(2,1)S(1)}, f32[16,2048]{1,0:T(8,128)S(1)}, f32[16,2048]{1,0:T(8,128)S(1)}, bf16[16,2048]{1,0:T(8,128)(2,1)}) custom-call(bf16[128,4096]{1,0:T(8,128)(2,1)S(1)} %collective-permute-done.halo, bf16[128,4096]{1,0:T(8,128)(2,1)S(1)} %get-tuple-element.56.product, bf16[128,4096]{1,0:T(8,128)(2,1)S(1)} %get-tuple-element.57.gate_mid, ...), custom_call_target="tpu_custom_call" | custom-call | flops 536870912 | bytes 8208384 | tf_op jit(solution)/shard_map/late/pallas_call | solution.py:279
  26.9 0.0 collective-permute-done.1.partner
  26.9 0.1 chip.1
  27.0 2.4 %collective-permute-start.2 = (bf16[16,2048]{1,0:T(8,128)(2,1)S(1)}, bf16[16,2048]{1,0:T(8,128)(2,1)S(1)}, u32[]{:S(2)}, u32[]{:S(2)}) collective-permute-start(bf16[16,2048]{1,0:T(8,128)(2,1)S(1)} %get-tuple-element.69), channel_id=1, source_target_pairs={{0,2},{1,3},{2,0},{3,1},{4,6},{5,7},{6,4},{7,5},{8,10},{9,11},{10,... | collective-permute-start | bytes 196616 | tf_op jit(solution)/shard_map/ppermute | solution.py:296
  29.4 2.2 %inner0.1 = (f32[256,1280]{1,0:T(8,128)S(1)}, bf16[128,1280]{1,0:T(8,128)(2,1)S(1)}, bf16[256,1280]{1,0:T(8,128)(2,1)S(1)}, f32[1,128]{1,0:T(1,128)S(1)}) custom-call(bf16[128,2048]{1,0:T(8,128)(2,1)S(1)} %get-tuple-element.72.other_a, bf16[128,2048]{1,0:T(8,128)(2,1)S(1)} %get-tuple-element.73.own_a, bf16[128,4096]{1,0:T(8,128)(2,1)S(1)} %get-tuple-element.74.gated_b, ...), custom_call_target="tpu_custom_call" | custom-call | flops 671088640 | bytes 6537728 | tf_op jit(solution)/shard_map/inner0/pallas_call | solution.py:279
  31.6 0.6 %collective-permute-done.2.received = bf16[16,2048]{1,0:T(8,128)(2,1)S(1)} collective-permute-done((bf16[16,2048]{1,0:T(8,128)(2,1)S(1)}, bf16[16,2048]{1,0:T(8,128)(2,1)S(1)}, u32[]{:S(2)}, u32[]{:S(2)}) %collective-permute-start.2) | collective-permute-done | bytes 65568 | tf_op jit(solution)/shard_map/ppermute | solution.py:296
  32.2 0.1 round.2
  32.3 2.8 %collective-permute-start.3 = (bf16[16,2048]{1,0:T(8,128)(2,1)S(1)}, bf16[16,2048]{1,0:T(8,128)(2,1)S(1)}, u32[]{:S(2)}, u32[]{:S(2)}) collective-permute-start(bf16[16,2048]{1,0:T(8,128)(2,1)S(1)} %get-tuple-element.80), channel_id=1, source_target_pairs={{0,4},{1,5},{2,6},{3,7},{4,0},{5,1},{6,2},{7,3},{8,12},{9,13},{10,... | collective-permute-start | bytes 196616 | tf_op jit(solution)/shard_map/ppermute | solution.py:296
  35.1 2.3 %inner1.1 = (f32[256,1408]{1,0:T(8,128)S(1)}, bf16[128,1408]{1,0:T(8,128)(2,1)S(1)}, bf16[256,1408]{1,0:T(8,128)(2,1)S(1)}, f32[1,128]{1,0:T(1,128)S(1)}) custom-call(bf16[128,2048]{1,0:T(8,128)(2,1)S(1)} %get-tuple-element.72.other_a, bf16[128,2048]{1,0:T(8,128)(2,1)S(1)} %get-tuple-element.73.own_a, bf16[128,4096]{1,0:T(8,128)(2,1)S(1)} %get-tuple-element.74.gated_b, ...), custom_call_target="tpu_custom_call" | custom-call | flops 738197504 | bytes 6767104 | tf_op jit(solution)/shard_map/inner1/pallas_call | solution.py:279
  37.4 0.0 collective-permute-done.3.received
  37.4 0.1 round.3
  37.5 3.0 %collective-permute-start.4 = (bf16[16,2048]{1,0:T(8,128)(2,1)S(1)}, bf16[16,2048]{1,0:T(8,128)(2,1)S(1)}, u32[]{:S(2)}, u32[]{:S(2)}) collective-permute-start(bf16[16,2048]{1,0:T(8,128)(2,1)S(1)} %get-tuple-element.86), channel_id=1, source_target_pairs={{0,8},{1,9},{2,10},{3,11},{4,12},{5,13},{6,14},{7,15},{8,0},{9,1},... | collective-permute-start | bytes 196616 | tf_op jit(solution)/shard_map/ppermute | solution.py:296
  40.5 2.3 %inner2.1 = (f32[256,1408]{1,0:T(8,128)S(1)}, bf16[128,1408]{1,0:T(8,128)(2,1)S(1)}, bf16[256,1408]{1,0:T(8,128)(2,1)S(1)}, f32[1,128]{1,0:T(1,128)S(1)}) custom-call(bf16[128,2048]{1,0:T(8,128)(2,1)S(1)} %get-tuple-element.72.other_a, bf16[128,2048]{1,0:T(8,128)(2,1)S(1)} %get-tuple-element.73.own_a, bf16[128,4096]{1,0:T(8,128)(2,1)S(1)} %get-tuple-element.74.gated_b, ...), custom_call_target="tpu_custom_call" | custom-call | flops 738197504 | bytes 6767104 | tf_op jit(solution)/shard_map/inner2/pallas_call | solution.py:279
  42.8 0.0 collective-permute-done.4.received
  42.8 0.1 last.1
  42.9 0.1 collective-permute-start.5
  43.0 1.2 %collective-permute-done.5.other = bf16[16,2048]{1,0:T(8,128)(2,1)S(1)} collective-permute-done((bf16[16,2048]{1,0:T(8,128)(2,1)S(1)}, bf16[16,2048]{1,0:T(8,128)(2,1)S(1)}, u32[]{:S(2)}, u32[]{:S(2)}) %collective-permute-start.5) | collective-permute-done | bytes 65568 | tf_op jit(solution)/shard_map/ppermute | solution.py:296
  44.3 1.8 %final.1 = bf16[256,4096]{1,0:T(8,128)(2,1)} custom-call(f32[16,2048]{1,0:T(8,128)S(1)} %get-tuple-element.90.own, bf16[16,2048]{1,0:T(8,128)(2,1)S(1)} %collective-permute-done.5.other, f32[16,2048]{1,0:T(8,128)S(1)} %get-tuple-element.92.own_state, f32[16,2048]{1,0:T(8,128)S(1)} %get-tuple-element.93.other_state, ...), custom_call_target="tpu_custom_call" | custom-call | flops 268435456 | bytes 10158080 | tf_op jit(solution)/shard_map/final/pallas_call | solution.py:279
  (6 shorter events, 0.0 us)
Async XLA Ops:
  0.0 4.2 %copy-start.3 = (f32[256,16]{0,1:T(8,128)S(1)}, f32[256,16]{0,1:T(8,128)}, u32[]{:S(2)}) copy-start(f32[256,16]{0,1:T(8,128)} %param.15) | copy-start | bytes 49156
  0.0 4.4 %copy-start.4 = (f32[256,16]{0,1:T(8,128)S(1)}, f32[256,16]{0,1:T(8,128)}, u32[]{:S(2)}) copy-start(f32[256,16]{0,1:T(8,128)} %param.16) | copy-start | bytes 49156
  0.0 4.6 %copy-start = (f32[4096]{0:T(1024)S(1)}, f32[4096]{0:T(1024)}, u32[]{:S(2)}) copy-start(f32[4096]{0:T(1024)} %param.14) | copy-start | bytes 49156
  0.0 4.6 %copy-start.2 = (bf16[256,128]{1,0:T(8,128)(2,1)S(1)}, bf16[256,128]{1,0:T(8,128)(2,1)}, u32[]{:S(2)}) copy-start(bf16[256,128]{1,0:T(8,128)(2,1)} %taps.1) | copy-start | bytes 196612
  1.7 12.1 %collective-permute-start = (bf16[128,4096]{1,0:T(8,128)(2,1)S(1)}, bf16[128,4096]{1,0:T(8,128)(2,1)S(1)}, u32[]{:S(2)}, u32[]{:S(2)}) collective-permute-start(bf16[128,4096]{1,0:T(8,128)(2,1)S(1)} %tail.1), channel_id=1, source_target_pairs={{0,1},{1,2},{2,3},{3,4},{4,5},{5,6},{6,7},{7,8},{8,9},{9,10},{10,1... | collective-permute-start | bytes 3145736 | tf_op jit(solution)/shard_map/ppermute | solution.py:394
  18.1 11.3 %copy-start.1 = (f32[4096]{0:T(1024)S(1)}, f32[4096]{0:T(1024)}, u32[]{:S(2)}) copy-start(f32[4096]{0:T(1024)} %param.17) | copy-start | bytes 49156
  18.1 8.8 %collective-permute-start.1 = (bf16[16,2048]{1,0:T(8,128)(2,1)S(1)}, bf16[16,2048]{1,0:T(8,128)(2,1)S(1)}, u32[]{:S(2)}, u32[]{:S(2)}) collective-permute-start(bf16[16,2048]{1,0:T(8,128)(2,1)S(1)} %get-tuple-element.65), channel_id=1, source_target_pairs={{0,1},{1,0},{2,3},{3,2},{4,5},{5,4},{6,7},{7,6},{8,9},{9,8},{10,11... | collective-permute-start | bytes 196616 | tf_op jit(solution)/shard_map/ppermute | solution.py:296
  27.0 5.2 %collective-permute-start.2 = (bf16[16,2048]{1,0:T(8,128)(2,1)S(1)}, bf16[16,2048]{1,0:T(8,128)(2,1)S(1)}, u32[]{:S(2)}, u32[]{:S(2)}) collective-permute-start(bf16[16,2048]{1,0:T(8,128)(2,1)S(1)} %get-tuple-element.69), channel_id=1, source_target_pairs={{0,2},{1,3},{2,0},{3,1},{4,6},{5,7},{6,4},{7,5},{8,10},{9,11},{10,... | collective-permute-start | bytes 196616 | tf_op jit(solution)/shard_map/ppermute | solution.py:296
  32.3 5.1 %collective-permute-start.3 = (bf16[16,2048]{1,0:T(8,128)(2,1)S(1)}, bf16[16,2048]{1,0:T(8,128)(2,1)S(1)}, u32[]{:S(2)}, u32[]{:S(2)}) collective-permute-start(bf16[16,2048]{1,0:T(8,128)(2,1)S(1)} %get-tuple-element.80), channel_id=1, source_target_pairs={{0,4},{1,5},{2,6},{3,7},{4,0},{5,1},{6,2},{7,3},{8,12},{9,13},{10,... | collective-permute-start | bytes 196616 | tf_op jit(solution)/shard_map/ppermute | solution.py:296
  37.5 5.3 %collective-permute-start.4 = (bf16[16,2048]{1,0:T(8,128)(2,1)S(1)}, bf16[16,2048]{1,0:T(8,128)(2,1)S(1)}, u32[]{:S(2)}, u32[]{:S(2)}) collective-permute-start(bf16[16,2048]{1,0:T(8,128)(2,1)S(1)} %get-tuple-element.86), channel_id=1, source_target_pairs={{0,8},{1,9},{2,10},{3,11},{4,12},{5,13},{6,14},{7,15},{8,0},{9,1},... | collective-permute-start | bytes 196616 | tf_op jit(solution)/shard_map/ppermute | solution.py:296
  42.9 1.3 %collective-permute-start.5 = (bf16[16,2048]{1,0:T(8,128)(2,1)S(1)}, bf16[16,2048]{1,0:T(8,128)(2,1)S(1)}, u32[]{:S(2)}, u32[]{:S(2)}) collective-permute-start(bf16[16,2048]{1,0:T(8,128)(2,1)S(1)} %get-tuple-element.91), channel_id=1, source_target_pairs={{0,1},{1,0},{2,3},{3,2},{4,5},{5,4},{6,7},{7,6},{8,9},{9,8},{10,11... | collective-permute-start | bytes 196616 | tf_op jit(solution)/shard_map/ppermute | solution.py:296

commit v4 on v3

--- a/solution.py
+++ b/solution.py
@@ -229,45 +229,55 @@
     return jnp.where(owner == mine, tall, 0.0).astype(BF16)
 
 
-def final_kernel(per_group, poles, own, other, own_state, other_state, rates_pc, *refs):
+def final_kernel(per_group, poles, followed, carry, state, rates_pc, *refs):
     parts, lifts, gates = (refs[k * PIECES : (k + 1) * PIECES] for k in range(3))
-    mixed, out, sems = refs[3 * PIECES :]
-    half = own.shape[1]
+    mixed, out, sems = refs[-3:]
+    half = carry.shape[1]
     upper = lax.axis_index("seq") % 2
-    copies = []
-    base = 0
-    for piece, (part, lift, gate) in enumerate(zip(parts, lifts, gates)):
-        width = part.shape[1]
-        for b in range(width // LANES):
-            at = slice(b * LANES, (b + 1) * LANES)
-            to = slice(base + b * LANES, base + (b + 1) * LANES)
-            side, inside = divmod(base + b * LANES, half)
-            inside = slice(inside, inside + LANES)
-            mine = upper == side
-            start = jnp.where(mine, own[:, inside], other[:, inside].astype(F32))
-            state = jnp.where(mine, own_state[:, inside], other_state[:, inside])
-            middle = jnp.exp(-rates_pc[:, to] * SUB) * start + state
+    places = [
+        (piece, b * LANES)
+        for piece, part in enumerate(parts)
+        for b in range(part.shape[1] // LANES)
+    ]
+
+    def write(side):
+        copies = []
+        for n in range(half // LANES):
+            piece, base = places[side * (half // LANES) + n]
+            at = slice(base, base + LANES)
+            here = slice(n * LANES, (n + 1) * LANES)
+            to = slice(side * half + n * LANES, side * half + (n + 1) * LANES)
+            start = carry[:, here].astype(F32)
+            middle = jnp.exp(-rates_pc[:, to] * SUB) * start + state[:, here]
             before = jnp.concatenate(
                 [spread_groups(start, per_group, poles), spread_groups(middle, per_group, poles)],
                 axis=1,
             )
-            lifted = dot(lift[:, at], before)
+            lifted = dot(lifts[piece][:, at], before)
             for k in range(2):
                 rows = slice(k * SUB, (k + 1) * SUB)
-                long_out = part[rows, at] + lifted[:, k * LANES : (k + 1) * LANES]
-                out[rows, to] = (gate[rows, at].astype(F32) * long_out).astype(BF16)
-        lanes = pl.ds(base, width)
-        copies.append(pltpu.make_async_copy(out.at[:, lanes], mixed.at[:, lanes], sems.at[piece]))
-        copies[-1].start()
-        base += width
-    for copy in copies:
-        copy.wait()
+                long_out = parts[piece][rows, at] + lifted[:, k * LANES : (k + 1) * LANES]
+                out[rows, here] = (gates[piece][rows, at].astype(F32) * long_out).astype(BF16)
+            if (n + 1) * LANES % CHUNK == 0:
+                first = (n + 1) * LANES - CHUNK
+                copy = pltpu.make_async_copy(
+                    out.at[:, pl.ds(first, CHUNK)],
+                    mixed.at[:, pl.ds(side * half + first, CHUNK)],
+                    sems.at[first // CHUNK],
+                )
+                copy.start()
+                copies.append(copy)
+        for copy in copies:
+            copy.wait()
+
+    for core in range(2):
+        pl.when(upper == core)(functools.partial(write, core if followed else 1 - core))
 
 
 HBM, VMEM, FREE = "hbm", "vmem", "free"
 
 
-def call(kernel, in_specs, outs, scratch, name, flops, args):
+def call(kernel, in_specs, outs, scratch, name, flops, args, aliases={}):
     moved = sum(a.size * a.dtype.itemsize for a in args)
     moved += sum(s.size * s.dtype.itemsize for s, _ in outs)
     spaces = {HBM: pltpu.HBM, VMEM: pltpu.VMEM}
@@ -284,6 +294,7 @@
             pltpu.VMEM(shape.shape, shape.dtype) if spec is VMEM else shape for shape, spec in outs
         ],
         scratch_shapes=scratch,
+        input_output_aliases=aliases,
         compiler_params=pltpu.CompilerParams(vmem_limit_bytes=20 << 20),
         cost_estimate=pl.CostEstimate(flops=flops, bytes_accessed=moved, transcendentals=0),
         name=name,
@@ -483,16 +494,22 @@
     while len(pieces) < PIECES:
         fill(other)
     parts, lifts, gates, _ = zip(*pieces)
-    (mixed,) = call(
-        functools.partial(final_kernel, per_group, poles),
-        [VMEM] * (5 + 3 * PIECES),
-        [(shape((row_count, features), BF16), HBM)],
-        [pltpu.VMEM((row_count, features), BF16), dma((PIECES,))],
-        "final",
-        2 * SUB * SUB * features * 2,
-        (carry, other, own_state, other_state, rates_pc, *parts, *lifts, *gates),
-    )
-    return mixed
+
+    def final(followed, carry, state, *earlier):
+        (mixed,) = call(
+            functools.partial(final_kernel, per_group, poles, followed),
+            [VMEM] * (3 + 3 * PIECES) + [HBM] * len(earlier),
+            [(shape((row_count, features), BF16), HBM)],
+            [pltpu.VMEM((row_count, features // 2), BF16), dma((chunks // 2,))],
+            "final",
+            SUB * SUB * features * 2,
+            (carry, state, rates_pc, *parts, *lifts, *gates, *earlier),
+            {3 + 3 * PIECES: 0} if earlier else {},
+        )
+        return mixed
+
+    mixed = final(True, carry, own_state)
+    return final(False, other, other_state, mixed)
 
 
 def solution(mesh):

time: 46.4 us -> 46 us (level)
  waiting for transfers between devices: 1.8 us -> 0.57 us
  Pallas kernels: 28.3 us -> 29.2 us
    ppermute x5, waiting for transfers between devices: 1.8 us -> 0.56 us  [swap(): return lax.ppermute(value, 'seq', route)]
    pallas_call x12 -> x13, Pallas kernels: 28.3 us -> 29.2 us  [call(): pl.pallas_call(kernel, in_specs=[where[spec] for spec in in_specs], out_s...]
  transfers between devices with their start and end apart: 6 -> 6, of which waited for: 2 -> 1; matrix products, arithmetic and copies ran while one was open for 1% -> 1% of each run, Pallas kernels for 44% -> 47%
where the time goes in v4:
time: 46 us; the launch traced here: 45.9 us
  Pallas kernels  29.2 us (63%)
  starting transfers between devices  15.4 us (33%)
  waiting for transfers between devices  0.57 us (1%)
    pallas_call x13, Pallas kernels, call(): pl.pallas_call(kernel, in_specs=[where[spec] for spec in in_specs], out_s...  29.2 us
    ppermute x5, starting transfers between devices, swap(): return lax.ppermute(value, 'seq', route)  12.9 us
    ppermute x1, starting transfers between devices, shards(): halo = lax.ppermute(tail, 'seq', [(i, i + 1) for i in range(count - 1)])  2.5 us
  transfers between devices with their start and end apart: 6, of which 1 were waited for; matrix products, arithmetic and copies ran while one was open for 1% of the time, Pallas kernels for 47%

profile of v4, /device:TPU:0, one launch (start us, length us, event | category | flops | bytes accessed | tf_op | source)
XLA Modules:
  0.0 45.9 jit_solution(16339740383724870161)
XLA Ops:
  0.0 1.7 %tail.1 = bf16[128,4096]{1,0:T(8,128)(2,1)S(1)} custom-call(bf16[256,4096]{1,0:T(8,128)(2,1)} %gate_in.3, bf16[256,4096]{1,0:T(8,128)(2,1)} %values.3), custom_call_target="tpu_custom_call" | custom-call | flops 524288 | bytes 5242880 | tf_op jit(solution)/shard_map/tail/pallas_call | solution.py:289
  1.7 2.5 %collective-permute-start = (bf16[128,4096]{1,0:T(8,128)(2,1)S(1)}, bf16[128,4096]{1,0:T(8,128)(2,1)S(1)}, u32[]{:S(2)}, u32[]{:S(2)}) collective-permute-start(bf16[128,4096]{1,0:T(8,128)(2,1)S(1)} %tail.1), channel_id=1, source_target_pairs={{0,1},{1,2},{2,3},{3,4},{4,5},{5,6},{6,7},{7,8},{8,9},{9,10},{10,1... | collective-permute-start | bytes 3145736 | tf_op jit(solution)/shard_map/ppermute | solution.py:405
  4.2 0.0 copy-done.3
  4.2 0.1 copy.14
  4.3 0.1 reshape.7.residues
  4.4 0.0 copy-done.4
  4.4 0.1 copy.13
  4.5 0.1 reshape.6.rates
  4.7 9.2 %early.1 = (bf16[8192,160]{1,0:T(8,128)(2,1)S(1)}, bf16[4096,128]{1,0:T(8,128)(2,1)S(1)}, f32[16,4096]{1,0:T(8,128)S(1)}, bf16[128,4096]{1,0:T(8,128)(2,1)S(1)},...) custom-call(bf16[256,4096]{1,0:T(8,128)(2,1)} %gate_in.3, ...), custom_call_target="tpu_custom_call" | custom-call | flops 1073741824 | bytes 13729792 | tf_op jit(solution)/shard_map/early/pallas_call | solution.py:289
  13.8 0.0 collective-permute-done.halo
  13.8 4.3 %late.2 = (bf16[128,2048]{1,0:T(8,128)(2,1)S(1)}, f32[16,2048]{1,0:T(8,128)S(1)}, f32[16,2048]{1,0:T(8,128)}, bf16[16,2048]{1,0:T(8,128)(2,1)S(1)}) custom-call(bf16[128,4096]{1,0:T(8,128)(2,1)S(1)} %collective-permute-done.halo, bf16[128,4096]{1,0:T(8,128)(2,1)S(1)} %get-tuple-element.56.product, bf16[128,4096]{1,0:T(8,128)(2,1)S(1)} %get-tuple-element.57.gate_mid, ...), custom_call_target="tpu_custom_call" | custom-call | flops 536870912 | bytes 8208384 | tf_op jit(solution)/shard_map/late/pallas_call | solution.py:289
  18.1 4.6 %collective-permute-start.1 = (bf16[16,2048]{1,0:T(8,128)(2,1)S(1)}, bf16[16,2048]{1,0:T(8,128)(2,1)S(1)}, u32[]{:S(2)}, u32[]{:S(2)}) collective-permute-start(bf16[16,2048]{1,0:T(8,128)(2,1)S(1)} %get-tuple-element.65), channel_id=1, source_target_pairs={{0,1},{1,0},{2,3},{3,2},{4,5},{5,4},{6,7},{7,6},{8,9},{9,8},{10,11... | collective-permute-start | bytes 196616 | tf_op jit(solution)/shard_map/ppermute | solution.py:307
  22.7 4.2 %late.3 = (bf16[128,2048]{1,0:T(8,128)(2,1)S(1)}, f32[16,2048]{1,0:T(8,128)S(1)}, f32[16,2048]{1,0:T(8,128)S(1)}, bf16[16,2048]{1,0:T(8,128)(2,1)}) custom-call(bf16[128,4096]{1,0:T(8,128)(2,1)S(1)} %collective-permute-done.halo, bf16[128,4096]{1,0:T(8,128)(2,1)S(1)} %get-tuple-element.56.product, bf16[128,4096]{1,0:T(8,128)(2,1)S(1)} %get-tuple-element.57.gate_mid, ...), custom_call_target="tpu_custom_call" | custom-call | flops 536870912 | bytes 8208384 | tf_op jit(solution)/shard_map/late/pallas_call | solution.py:289
  26.9 0.0 collective-permute-done.1.partner
  26.9 0.1 chip.1
  27.0 2.4 %collective-permute-start.2 = (bf16[16,2048]{1,0:T(8,128)(2,1)S(1)}, bf16[16,2048]{1,0:T(8,128)(2,1)S(1)}, u32[]{:S(2)}, u32[]{:S(2)}) collective-permute-start(bf16[16,2048]{1,0:T(8,128)(2,1)S(1)} %get-tuple-element.69), channel_id=1, source_target_pairs={{0,2},{1,3},{2,0},{3,1},{4,6},{5,7},{6,4},{7,5},{8,10},{9,11},{10,... | collective-permute-start | bytes 196616 | tf_op jit(solution)/shard_map/ppermute | solution.py:307
  29.4 0.0 copy-done.1
  29.4 2.2 %inner0.1 = (f32[256,1280]{1,0:T(8,128)S(1)}, bf16[128,1280]{1,0:T(8,128)(2,1)S(1)}, bf16[256,1280]{1,0:T(8,128)(2,1)S(1)}, f32[1,128]{1,0:T(1,128)S(1)}) custom-call(bf16[128,2048]{1,0:T(8,128)(2,1)S(1)} %get-tuple-element.72.other_a, bf16[128,2048]{1,0:T(8,128)(2,1)S(1)} %get-tuple-element.73.own_a, bf16[128,4096]{1,0:T(8,128)(2,1)S(1)} %get-tuple-element.74.gated_b, ...), custom_call_target="tpu_custom_call" | custom-call | flops 671088640 | bytes 6537728 | tf_op jit(solution)/shard_map/inner0/pallas_call | solution.py:289
  31.6 0.6 %collective-permute-done.2.received = bf16[16,2048]{1,0:T(8,128)(2,1)S(1)} collective-permute-done((bf16[16,2048]{1,0:T(8,128)(2,1)S(1)}, bf16[16,2048]{1,0:T(8,128)(2,1)S(1)}, u32[]{:S(2)}, u32[]{:S(2)}) %collective-permute-start.2) | collective-permute-done | bytes 65568 | tf_op jit(solution)/shard_map/ppermute | solution.py:307
  32.2 0.1 round.2
  32.3 2.8 %collective-permute-start.3 = (bf16[16,2048]{1,0:T(8,128)(2,1)S(1)}, bf16[16,2048]{1,0:T(8,128)(2,1)S(1)}, u32[]{:S(2)}, u32[]{:S(2)}) collective-permute-start(bf16[16,2048]{1,0:T(8,128)(2,1)S(1)} %get-tuple-element.80), channel_id=1, source_target_pairs={{0,4},{1,5},{2,6},{3,7},{4,0},{5,1},{6,2},{7,3},{8,12},{9,13},{10,... | collective-permute-start | bytes 196616 | tf_op jit(solution)/shard_map/ppermute | solution.py:307
  35.1 2.3 %inner1.1 = (f32[256,1408]{1,0:T(8,128)S(1)}, bf16[128,1408]{1,0:T(8,128)(2,1)S(1)}, bf16[256,1408]{1,0:T(8,128)(2,1)S(1)}, f32[1,128]{1,0:T(1,128)S(1)}) custom-call(bf16[128,2048]{1,0:T(8,128)(2,1)S(1)} %get-tuple-element.72.other_a, bf16[128,2048]{1,0:T(8,128)(2,1)S(1)} %get-tuple-element.73.own_a, bf16[128,4096]{1,0:T(8,128)(2,1)S(1)} %get-tuple-element.74.gated_b, ...), custom_call_target="tpu_custom_call" | custom-call | flops 738197504 | bytes 6767104 | tf_op jit(solution)/shard_map/inner1/pallas_call | solution.py:289
  37.4 0.0 collective-permute-done.3.received
  37.4 0.1 round.3
  37.5 3.0 %collective-permute-start.4 = (bf16[16,2048]{1,0:T(8,128)(2,1)S(1)}, bf16[16,2048]{1,0:T(8,128)(2,1)S(1)}, u32[]{:S(2)}, u32[]{:S(2)}) collective-permute-start(bf16[16,2048]{1,0:T(8,128)(2,1)S(1)} %get-tuple-element.86), channel_id=1, source_target_pairs={{0,8},{1,9},{2,10},{3,11},{4,12},{5,13},{6,14},{7,15},{8,0},{9,1},... | collective-permute-start | bytes 196616 | tf_op jit(solution)/shard_map/ppermute | solution.py:307
  40.5 2.3 %inner2.1 = (f32[256,1408]{1,0:T(8,128)S(1)}, bf16[128,1408]{1,0:T(8,128)(2,1)S(1)}, bf16[256,1408]{1,0:T(8,128)(2,1)S(1)}, f32[1,128]{1,0:T(1,128)S(1)}) custom-call(bf16[128,2048]{1,0:T(8,128)(2,1)S(1)} %get-tuple-element.72.other_a, bf16[128,2048]{1,0:T(8,128)(2,1)S(1)} %get-tuple-element.73.own_a, bf16[128,4096]{1,0:T(8,128)(2,1)S(1)} %get-tuple-element.74.gated_b, ...), custom_call_target="tpu_custom_call" | custom-call | flops 738197504 | bytes 6767104 | tf_op jit(solution)/shard_map/inner2/pallas_call | solution.py:289
  42.8 0.0 collective-permute-done.4.received
  42.8 0.1 last.1
  42.9 0.1 collective-permute-start.5
  43.0 1.3 %final.2.refs_9_ = bf16[256,4096]{1,0:T(8,128)(2,1)} custom-call(f32[16,2048]{1,0:T(8,128)S(1)} %get-tuple-element.101.carry, f32[16,2048]{1,0:T(8,128)S(1)} %get-tuple-element.102.state, f32[16,4096]{1,0:T(8,128)S(1)} %get-tuple-element.60.rates_pc, f32[256,1280]{1,0:T(8,128)S(1)} %get-tuple-element.92.refs_0_, f32[256,1408]{1,0:T(8,128)S(1)} %get-tuple-element.93.refs_1_, ...), custom_call_target="tpu_custom_call" | custom-call | flops 134217728 | bytes 9961472 | tf_op jit(solution)/shard_map/final/pallas_call | solution.py:289
  44.4 0.0 collective-permute-done.5.carry
  44.4 1.3 %final.3 = bf16[256,4096]{1,0:T(8,128)(2,1)} custom-call(bf16[16,2048]{1,0:T(8,128)(2,1)S(1)} %collective-permute-done.5.carry, f32[16,2048]{1,0:T(8,128)S(1)} %get-tuple-element.91.state, f32[16,4096]{1,0:T(8,128)S(1)} %get-tuple-element.60.rates_pc, f32[256,1280]{1,0:T(8,128)S(1)} %get-tuple-element.92.refs_0_, ...), custom_call_target="tpu_custom_call", output_to_operand_aliasing={{}: (12, {})} | custom-call | flops 134217728 | bytes 11993088 | tf_op jit(solution)/shard_map/final/pallas_call | solution.py:289
  (7 shorter events, 0.0 us)
Async XLA Ops:
  0.0 4.2 %copy-start.3 = (f32[256,16]{0,1:T(8,128)S(1)}, f32[256,16]{0,1:T(8,128)}, u32[]{:S(2)}) copy-start(f32[256,16]{0,1:T(8,128)} %param.15) | copy-start | bytes 49156
  0.0 4.4 %copy-start.4 = (f32[256,16]{0,1:T(8,128)S(1)}, f32[256,16]{0,1:T(8,128)}, u32[]{:S(2)}) copy-start(f32[256,16]{0,1:T(8,128)} %param.16) | copy-start | bytes 49156
  0.0 4.6 %copy-start = (f32[4096]{0:T(1024)S(1)}, f32[4096]{0:T(1024)}, u32[]{:S(2)}) copy-start(f32[4096]{0:T(1024)} %param.14) | copy-start | bytes 49156
  0.0 4.6 %copy-start.2 = (bf16[256,128]{1,0:T(8,128)(2,1)S(1)}, bf16[256,128]{1,0:T(8,128)(2,1)}, u32[]{:S(2)}) copy-start(bf16[256,128]{1,0:T(8,128)(2,1)} %taps.1) | copy-start | bytes 196612
  1.7 12.1 %collective-permute-start = (bf16[128,4096]{1,0:T(8,128)(2,1)S(1)}, bf16[128,4096]{1,0:T(8,128)(2,1)S(1)}, u32[]{:S(2)}, u32[]{:S(2)}) collective-permute-start(bf16[128,4096]{1,0:T(8,128)(2,1)S(1)} %tail.1), channel_id=1, source_target_pairs={{0,1},{1,2},{2,3},{3,4},{4,5},{5,6},{6,7},{7,8},{8,9},{9,10},{10,1... | collective-permute-start | bytes 3145736 | tf_op jit(solution)/shard_map/ppermute | solution.py:405
  18.1 11.3 %copy-start.1 = (f32[4096]{0:T(1024)S(1)}, f32[4096]{0:T(1024)}, u32[]{:S(2)}) copy-start(f32[4096]{0:T(1024)} %param.17) | copy-start | bytes 49156
  18.1 8.8 %collective-permute-start.1 = (bf16[16,2048]{1,0:T(8,128)(2,1)S(1)}, bf16[16,2048]{1,0:T(8,128)(2,1)S(1)}, u32[]{:S(2)}, u32[]{:S(2)}) collective-permute-start(bf16[16,2048]{1,0:T(8,128)(2,1)S(1)} %get-tuple-element.65), channel_id=1, source_target_pairs={{0,1},{1,0},{2,3},{3,2},{4,5},{5,4},{6,7},{7,6},{8,9},{9,8},{10,11... | collective-permute-start | bytes 196616 | tf_op jit(solution)/shard_map/ppermute | solution.py:307
  27.0 5.2 %collective-permute-start.2 = (bf16[16,2048]{1,0:T(8,128)(2,1)S(1)}, bf16[16,2048]{1,0:T(8,128)(2,1)S(1)}, u32[]{:S(2)}, u32[]{:S(2)}) collective-permute-start(bf16[16,2048]{1,0:T(8,128)(2,1)S(1)} %get-tuple-element.69), channel_id=1, source_target_pairs={{0,2},{1,3},{2,0},{3,1},{4,6},{5,7},{6,4},{7,5},{8,10},{9,11},{10,... | collective-permute-start | bytes 196616 | tf_op jit(solution)/shard_map/ppermute | solution.py:307
  32.3 5.1 %collective-permute-start.3 = (bf16[16,2048]{1,0:T(8,128)(2,1)S(1)}, bf16[16,2048]{1,0:T(8,128)(2,1)S(1)}, u32[]{:S(2)}, u32[]{:S(2)}) collective-permute-start(bf16[16,2048]{1,0:T(8,128)(2,1)S(1)} %get-tuple-element.80), channel_id=1, source_target_pairs={{0,4},{1,5},{2,6},{3,7},{4,0},{5,1},{6,2},{7,3},{8,12},{9,13},{10,... | collective-permute-start | bytes 196616 | tf_op jit(solution)/shard_map/ppermute | solution.py:307
  37.5 5.3 %collective-permute-start.4 = (bf16[16,2048]{1,0:T(8,128)(2,1)S(1)}, bf16[16,2048]{1,0:T(8,128)(2,1)S(1)}, u32[]{:S(2)}, u32[]{:S(2)}) collective-permute-start(bf16[16,2048]{1,0:T(8,128)(2,1)S(1)} %get-tuple-element.86), channel_id=1, source_target_pairs={{0,8},{1,9},{2,10},{3,11},{4,12},{5,13},{6,14},{7,15},{8,0},{9,1},... | collective-permute-start | bytes 196616 | tf_op jit(solution)/shard_map/ppermute | solution.py:307
  42.9 1.4 %collective-permute-start.5 = (bf16[16,2048]{1,0:T(8,128)(2,1)S(1)}, bf16[16,2048]{1,0:T(8,128)(2,1)S(1)}, u32[]{:S(2)}, u32[]{:S(2)}) collective-permute-start(bf16[16,2048]{1,0:T(8,128)(2,1)S(1)} %get-tuple-element.90), channel_id=1, source_target_pairs={{0,1},{1,0},{2,3},{3,2},{4,5},{5,4},{6,7},{7,6},{8,9},{9,8},{10,11... | collective-permute-start | bytes 196616 | tf_op jit(solution)/shard_map/ppermute | solution.py:307

commit v5 on v4

--- a/solution.py
+++ b/solution.py
@@ -388,7 +388,7 @@
     groups, poles = rates.shape
     per_group = features // groups
     count = lax.axis_size("seq")
-    cuts = [features // LANES * k // PIECES * LANES for k in range(PIECES + 1)]
+    cuts = [features // LANES * k // 32 * LANES for k in (0, 12, 22, 32)]
     shape = jax.ShapeDtypeStruct
     dma = pltpu.SemaphoreType.DMA
     chunks = features // CHUNK

time: 46 us -> 46 us (level)
  transfers between devices with their start and end apart: 6 -> 6, of which waited for: 1 -> 2; matrix products, arithmetic and copies ran while one was open for 1% -> 1% of each run, Pallas kernels for 47% -> 47%
where the time goes in v5:
time: 46 us; the launch traced here: 45.7 us
  Pallas kernels  29.1 us (63%)
  starting transfers between devices  15.5 us (34%)
    pallas_call x13, Pallas kernels, call(): pl.pallas_call(kernel, in_specs=[where[spec] for spec in in_specs], out_s...  29.1 us
    ppermute x5, starting transfers between devices, swap(): return lax.ppermute(value, 'seq', route)  13 us
    ppermute x1, starting transfers between devices, shards(): halo = lax.ppermute(tail, 'seq', [(i, i + 1) for i in range(count - 1)])  2.5 us
  transfers between devices with their start and end apart: 6, of which 2 were waited for; matrix products, arithmetic and copies ran while one was open for 1% of the time, Pallas kernels for 47%

profile of v5, /device:TPU:0, one launch (start us, length us, event | category | flops | bytes accessed | tf_op | source)
XLA Modules:
  0.0 45.7 jit_solution(1507622321119087906)
XLA Ops:
  0.0 1.7 %tail.1 = bf16[128,4096]{1,0:T(8,128)(2,1)S(1)} custom-call(bf16[256,4096]{1,0:T(8,128)(2,1)} %gate_in.3, bf16[256,4096]{1,0:T(8,128)(2,1)} %values.3), custom_call_target="tpu_custom_call" | custom-call | flops 524288 | bytes 5242880 | tf_op jit(solution)/shard_map/tail/pallas_call | solution.py:289
  1.7 2.5 %collective-permute-start = (bf16[128,4096]{1,0:T(8,128)(2,1)S(1)}, bf16[128,4096]{1,0:T(8,128)(2,1)S(1)}, u32[]{:S(2)}, u32[]{:S(2)}) collective-permute-start(bf16[128,4096]{1,0:T(8,128)(2,1)S(1)} %tail.1), channel_id=1, source_target_pairs={{0,1},{1,2},{2,3},{3,4},{4,5},{5,6},{6,7},{7,8},{8,9},{9,10},{10,1... | collective-permute-start | bytes 3145736 | tf_op jit(solution)/shard_map/ppermute | solution.py:405
  4.2 0.0 copy-done.3
  4.2 0.1 copy.14
  4.3 0.1 reshape.7.residues
  4.4 0.0 copy-done.4
  4.4 0.1 copy.13
  4.5 0.1 reshape.6.rates
  4.7 9.2 %early.1 = (bf16[8192,160]{1,0:T(8,128)(2,1)S(1)}, bf16[4096,128]{1,0:T(8,128)(2,1)S(1)}, f32[16,4096]{1,0:T(8,128)S(1)}, bf16[128,4096]{1,0:T(8,128)(2,1)S(1)},...) custom-call(bf16[256,4096]{1,0:T(8,128)(2,1)} %gate_in.3, ...), custom_call_target="tpu_custom_call" | custom-call | flops 1073741824 | bytes 13729792 | tf_op jit(solution)/shard_map/early/pallas_call | solution.py:289
  13.8 0.0 collective-permute-done.halo
  13.8 4.3 %late.2 = (bf16[128,2048]{1,0:T(8,128)(2,1)S(1)}, f32[16,2048]{1,0:T(8,128)S(1)}, f32[16,2048]{1,0:T(8,128)}, bf16[16,2048]{1,0:T(8,128)(2,1)S(1)}) custom-call(bf16[128,4096]{1,0:T(8,128)(2,1)S(1)} %collective-permute-done.halo, bf16[128,4096]{1,0:T(8,128)(2,1)S(1)} %get-tuple-element.56.product, bf16[128,4096]{1,0:T(8,128)(2,1)S(1)} %get-tuple-element.57.gate_mid, ...), custom_call_target="tpu_custom_call" | custom-call | flops 536870912 | bytes 8208384 | tf_op jit(solution)/shard_map/late/pallas_call | solution.py:289
  18.1 4.6 %collective-permute-start.1 = (bf16[16,2048]{1,0:T(8,128)(2,1)S(1)}, bf16[16,2048]{1,0:T(8,128)(2,1)S(1)}, u32[]{:S(2)}, u32[]{:S(2)}) collective-permute-start(bf16[16,2048]{1,0:T(8,128)(2,1)S(1)} %get-tuple-element.65), channel_id=1, source_target_pairs={{0,1},{1,0},{2,3},{3,2},{4,5},{5,4},{6,7},{7,6},{8,9},{9,8},{10,11... | collective-permute-start | bytes 196616 | tf_op jit(solution)/shard_map/ppermute | solution.py:307
  22.7 4.2 %late.3 = (bf16[128,2048]{1,0:T(8,128)(2,1)S(1)}, f32[16,2048]{1,0:T(8,128)S(1)}, f32[16,2048]{1,0:T(8,128)S(1)}, bf16[16,2048]{1,0:T(8,128)(2,1)}) custom-call(bf16[128,4096]{1,0:T(8,128)(2,1)S(1)} %collective-permute-done.halo, bf16[128,4096]{1,0:T(8,128)(2,1)S(1)} %get-tuple-element.56.product, bf16[128,4096]{1,0:T(8,128)(2,1)S(1)} %get-tuple-element.57.gate_mid, ...), custom_call_target="tpu_custom_call" | custom-call | flops 536870912 | bytes 8208384 | tf_op jit(solution)/shard_map/late/pallas_call | solution.py:289
  26.9 0.0 collective-permute-done.1.partner
  26.9 0.1 chip.1
  27.0 2.4 %collective-permute-start.2 = (bf16[16,2048]{1,0:T(8,128)(2,1)S(1)}, bf16[16,2048]{1,0:T(8,128)(2,1)S(1)}, u32[]{:S(2)}, u32[]{:S(2)}) collective-permute-start(bf16[16,2048]{1,0:T(8,128)(2,1)S(1)} %get-tuple-element.69), channel_id=1, source_target_pairs={{0,2},{1,3},{2,0},{3,1},{4,6},{5,7},{6,4},{7,5},{8,10},{9,11},{10,... | collective-permute-start | bytes 196616 | tf_op jit(solution)/shard_map/ppermute | solution.py:307
  29.4 0.0 copy-done.1
  29.4 2.7 %inner0.1 = (f32[256,1536]{1,0:T(8,128)S(1)}, bf16[128,1536]{1,0:T(8,128)(2,1)S(1)}, bf16[256,1536]{1,0:T(8,128)(2,1)S(1)}, f32[1,128]{1,0:T(1,128)S(1)}) custom-call(bf16[128,2048]{1,0:T(8,128)(2,1)S(1)} %get-tuple-element.72.other_a, bf16[128,2048]{1,0:T(8,128)(2,1)S(1)} %get-tuple-element.73.own_a, bf16[128,4096]{1,0:T(8,128)(2,1)S(1)} %get-tuple-element.74.gated_b, ...), custom_call_target="tpu_custom_call" | custom-call | flops 805306368 | bytes 6996480 | tf_op jit(solution)/shard_map/inner0/pallas_call | solution.py:289
  32.2 0.0 collective-permute-done.2.received
  32.2 0.1 round.2
  32.3 2.8 %collective-permute-start.3 = (bf16[16,2048]{1,0:T(8,128)(2,1)S(1)}, bf16[16,2048]{1,0:T(8,128)(2,1)S(1)}, u32[]{:S(2)}, u32[]{:S(2)}) collective-permute-start(bf16[16,2048]{1,0:T(8,128)(2,1)S(1)} %get-tuple-element.80), channel_id=1, source_target_pairs={{0,4},{1,5},{2,6},{3,7},{4,0},{5,1},{6,2},{7,3},{8,12},{9,13},{10,... | collective-permute-start | bytes 196616 | tf_op jit(solution)/shard_map/ppermute | solution.py:307
  35.1 2.0 %inner1.1 = (f32[256,1280]{1,0:T(8,128)S(1)}, bf16[128,1280]{1,0:T(8,128)(2,1)S(1)}, bf16[256,1280]{1,0:T(8,128)(2,1)S(1)}, f32[1,128]{1,0:T(1,128)S(1)}) custom-call(bf16[128,2048]{1,0:T(8,128)(2,1)S(1)} %get-tuple-element.72.other_a, bf16[128,2048]{1,0:T(8,128)(2,1)S(1)} %get-tuple-element.73.own_a, bf16[128,4096]{1,0:T(8,128)(2,1)S(1)} %get-tuple-element.74.gated_b, ...), custom_call_target="tpu_custom_call" | custom-call | flops 671088640 | bytes 6537728 | tf_op jit(solution)/shard_map/inner1/pallas_call | solution.py:289
  37.1 0.2 collective-permute-done.3.received
  37.3 0.1 round.3
  37.4 3.1 %collective-permute-start.4 = (bf16[16,2048]{1,0:T(8,128)(2,1)S(1)}, bf16[16,2048]{1,0:T(8,128)(2,1)S(1)}, u32[]{:S(2)}, u32[]{:S(2)}) collective-permute-start(bf16[16,2048]{1,0:T(8,128)(2,1)S(1)} %get-tuple-element.86), channel_id=1, source_target_pairs={{0,8},{1,9},{2,10},{3,11},{4,12},{5,13},{6,14},{7,15},{8,0},{9,1},... | collective-permute-start | bytes 196616 | tf_op jit(solution)/shard_map/ppermute | solution.py:307
  40.5 2.0 %inner2.1 = (f32[256,1280]{1,0:T(8,128)S(1)}, bf16[128,1280]{1,0:T(8,128)(2,1)S(1)}, bf16[256,1280]{1,0:T(8,128)(2,1)S(1)}, f32[1,128]{1,0:T(1,128)S(1)}) custom-call(bf16[128,2048]{1,0:T(8,128)(2,1)S(1)} %get-tuple-element.72.other_a, bf16[128,2048]{1,0:T(8,128)(2,1)S(1)} %get-tuple-element.73.own_a, bf16[128,4096]{1,0:T(8,128)(2,1)S(1)} %get-tuple-element.74.gated_b, ...), custom_call_target="tpu_custom_call" | custom-call | flops 671088640 | bytes 6537728 | tf_op jit(solution)/shard_map/inner2/pallas_call | solution.py:289
  42.5 0.2 collective-permute-done.4.received
  42.7 0.1 last.1
  42.8 0.1 collective-permute-start.5
  42.9 1.3 %final.2.refs_9_ = bf16[256,4096]{1,0:T(8,128)(2,1)} custom-call(f32[16,2048]{1,0:T(8,128)S(1)} %get-tuple-element.101.carry, f32[16,2048]{1,0:T(8,128)S(1)} %get-tuple-element.102.state, f32[16,4096]{1,0:T(8,128)S(1)} %get-tuple-element.60.rates_pc, f32[256,1536]{1,0:T(8,128)S(1)} %get-tuple-element.92.refs_0_, f32[256,1280]{1,0:T(8,128)S(1)} %get-tuple-element.93.refs_1_, ...), custom_call_target="tpu_custom_call" | custom-call | flops 134217728 | bytes 9961472 | tf_op jit(solution)/shard_map/final/pallas_call | solution.py:289
  44.2 0.0 collective-permute-done.5.carry
  44.3 1.3 %final.3 = bf16[256,4096]{1,0:T(8,128)(2,1)} custom-call(bf16[16,2048]{1,0:T(8,128)(2,1)S(1)} %collective-permute-done.5.carry, f32[16,2048]{1,0:T(8,128)S(1)} %get-tuple-element.91.state, f32[16,4096]{1,0:T(8,128)S(1)} %get-tuple-element.60.rates_pc, f32[256,1536]{1,0:T(8,128)S(1)} %get-tuple-element.92.refs_0_, ...), custom_call_target="tpu_custom_call", output_to_operand_aliasing={{}: (12, {})} | custom-call | flops 134217728 | bytes 11993088 | tf_op jit(solution)/shard_map/final/pallas_call | solution.py:289
  (7 shorter events, 0.0 us)
Async XLA Ops:
  0.0 4.2 %copy-start.3 = (f32[256,16]{0,1:T(8,128)S(1)}, f32[256,16]{0,1:T(8,128)}, u32[]{:S(2)}) copy-start(f32[256,16]{0,1:T(8,128)} %param.15) | copy-start | bytes 49156
  0.0 4.4 %copy-start.4 = (f32[256,16]{0,1:T(8,128)S(1)}, f32[256,16]{0,1:T(8,128)}, u32[]{:S(2)}) copy-start(f32[256,16]{0,1:T(8,128)} %param.16) | copy-start | bytes 49156
  0.0 4.6 %copy-start = (f32[4096]{0:T(1024)S(1)}, f32[4096]{0:T(1024)}, u32[]{:S(2)}) copy-start(f32[4096]{0:T(1024)} %param.14) | copy-start | bytes 49156
  0.0 4.6 %copy-start.2 = (bf16[256,128]{1,0:T(8,128)(2,1)S(1)}, bf16[256,128]{1,0:T(8,128)(2,1)}, u32[]{:S(2)}) copy-start(bf16[256,128]{1,0:T(8,128)(2,1)} %taps.1) | copy-start | bytes 196612
  1.7 12.1 %collective-permute-start = (bf16[128,4096]{1,0:T(8,128)(2,1)S(1)}, bf16[128,4096]{1,0:T(8,128)(2,1)S(1)}, u32[]{:S(2)}, u32[]{:S(2)}) collective-permute-start(bf16[128,4096]{1,0:T(8,128)(2,1)S(1)} %tail.1), channel_id=1, source_target_pairs={{0,1},{1,2},{2,3},{3,4},{4,5},{5,6},{6,7},{7,8},{8,9},{9,10},{10,1... | collective-permute-start | bytes 3145736 | tf_op jit(solution)/shard_map/ppermute | solution.py:405
  18.1 11.3 %copy-start.1 = (f32[4096]{0:T(1024)S(1)}, f32[4096]{0:T(1024)}, u32[]{:S(2)}) copy-start(f32[4096]{0:T(1024)} %param.17) | copy-start | bytes 49156
  18.1 8.8 %collective-permute-start.1 = (bf16[16,2048]{1,0:T(8,128)(2,1)S(1)}, bf16[16,2048]{1,0:T(8,128)(2,1)S(1)}, u32[]{:S(2)}, u32[]{:S(2)}) collective-permute-start(bf16[16,2048]{1,0:T(8,128)(2,1)S(1)} %get-tuple-element.65), channel_id=1, source_target_pairs={{0,1},{1,0},{2,3},{3,2},{4,5},{5,4},{6,7},{7,6},{8,9},{9,8},{10,11... | collective-permute-start | bytes 196616 | tf_op jit(solution)/shard_map/ppermute | solution.py:307
  27.0 5.2 %collective-permute-start.2 = (bf16[16,2048]{1,0:T(8,128)(2,1)S(1)}, bf16[16,2048]{1,0:T(8,128)(2,1)S(1)}, u32[]{:S(2)}, u32[]{:S(2)}) collective-permute-start(bf16[16,2048]{1,0:T(8,128)(2,1)S(1)} %get-tuple-element.69), channel_id=1, source_target_pairs={{0,2},{1,3},{2,0},{3,1},{4,6},{5,7},{6,4},{7,5},{8,10},{9,11},{10,... | collective-permute-start | bytes 196616 | tf_op jit(solution)/shard_map/ppermute | solution.py:307
  32.3 5.0 %collective-permute-start.3 = (bf16[16,2048]{1,0:T(8,128)(2,1)S(1)}, bf16[16,2048]{1,0:T(8,128)(2,1)S(1)}, u32[]{:S(2)}, u32[]{:S(2)}) collective-permute-start(bf16[16,2048]{1,0:T(8,128)(2,1)S(1)} %get-tuple-element.80), channel_id=1, source_target_pairs={{0,4},{1,5},{2,6},{3,7},{4,0},{5,1},{6,2},{7,3},{8,12},{9,13},{10,... | collective-permute-start | bytes 196616 | tf_op jit(solution)/shard_map/ppermute | solution.py:307
  37.4 5.3 %collective-permute-start.4 = (bf16[16,2048]{1,0:T(8,128)(2,1)S(1)}, bf16[16,2048]{1,0:T(8,128)(2,1)S(1)}, u32[]{:S(2)}, u32[]{:S(2)}) collective-permute-start(bf16[16,2048]{1,0:T(8,128)(2,1)S(1)} %get-tuple-element.86), channel_id=1, source_target_pairs={{0,8},{1,9},{2,10},{3,11},{4,12},{5,13},{6,14},{7,15},{8,0},{9,1},... | collective-permute-start | bytes 196616 | tf_op jit(solution)/shard_map/ppermute | solution.py:307
  42.8 1.4 %collective-permute-start.5 = (bf16[16,2048]{1,0:T(8,128)(2,1)S(1)}, bf16[16,2048]{1,0:T(8,128)(2,1)S(1)}, u32[]{:S(2)}, u32[]{:S(2)}) collective-permute-start(bf16[16,2048]{1,0:T(8,128)(2,1)S(1)} %get-tuple-element.90), channel_id=1, source_target_pairs={{0,1},{1,0},{2,3},{3,2},{4,5},{5,4},{6,7},{7,6},{8,9},{9,8},{10,11... | collective-permute-start | bytes 196616 | tf_op jit(solution)/shard_map/ppermute | solution.py:307
